TPU v7x, 32 devices: a whole 2x2x4 slice. The times are simulated.
32 devices in a mesh: blk: 4 (over z), seq: 2 (over y), shard: 4 (over x, core).
Axes of the slice: x: 2, y: 2, z: 4, core: 2. Of those that a mesh axis runs over, the one named last changes fastest.
Arguments:
- tokens: bfloat16 [8, 2048, 768], P(('seq', 'shard'), 'blk'), may hold values from -6 to 6
- segments: int32 [8, 2048], P(('seq', 'shard')), may hold values from 0 to 2047, as said below
- live_mask: int32 [8, 2048], P(('seq', 'shard')), may hold values from 0 to 1, as said below
- query_weight: bfloat16 [768, 768], P(('seq', 'shard')), may hold values from -0.21875 to 0.21875
- key_weight: bfloat16 [768, 768], P(('seq', 'shard')), may hold values from -0.21875 to 0.21875
- value_weight: bfloat16 [768, 768], P(('seq', 'shard')), may hold values from -0.21875 to 0.21875
- out_weight: bfloat16 [768, 768], P(('seq', 'shard')), may hold values from -6 to 6
- query_bias: bfloat16 [768], P(('seq', 'shard')), may hold values from -1 to 1
- value_bias: bfloat16 [768], P(('seq', 'shard')), may hold values from -1 to 1
- out_bias: bfloat16 [768], P(('seq', 'shard')), may hold values from -1 to 1
- first_gain: bfloat16 [768], P(('seq', 'shard')), may hold values from 0.5 to 1.5
- first_shift: bfloat16 [768], P(('seq', 'shard')), may hold values from -1 to 1
- up_weight: bfloat16 [768, 3072], P(('seq', 'shard')), may hold values from -0.21875 to 0.21875
- up_bias: bfloat16 [3072], P(('seq', 'shard')), may hold values from -1 to 1
- down_weight: bfloat16 [3072, 768], P(('seq', 'shard')), may hold values from -0.109375 to 0.109375
- down_bias: bfloat16 [768], P(('seq', 'shard')), may hold values from -1 to 1
- second_gain: bfloat16 [768], P(('seq', 'shard')), may hold values from 0.5 to 1.5
- second_shift: bfloat16 [768], P(('seq', 'shard')), may hold values from -1 to 1
- cotangent: bfloat16 [8, 2048, 768], P(('seq', 'shard'), 'blk'), may hold values from -6 to 6
Outputs:
- layer_out: bfloat16 [8, 2048, 768], P(('seq', 'shard'), 'blk')
- token_grad: bfloat16 [8, 2048, 768], P(('seq', 'shard'), 'blk')
- query_weight_grad: float32 [768, 768], P(('seq', 'shard'))
- key_weight_grad: float32 [768, 768], P(('seq', 'shard'))
- value_weight_grad: float32 [768, 768], P(('seq', 'shard'))
- out_weight_grad: float32 [768, 768], P(('seq', 'shard'))
- query_bias_grad: float32 [768], P(('seq', 'shard'))
- value_bias_grad: float32 [768], P(('seq', 'shard'))
- out_bias_grad: float32 [768], P(('seq', 'shard'))
- first_gain_grad: float32 [768], P(('seq', 'shard'))
- first_shift_grad: float32 [768], P(('seq', 'shard'))
- up_weight_grad: float32 [768, 3072], P(('seq', 'shard'))
- up_bias_grad: float32 [3072], P(('seq', 'shard'))
- down_weight_grad: float32 [3072, 768], P(('seq', 'shard'))
- down_bias_grad: float32 [768], P(('seq', 'shard'))
- second_gain_grad: float32 [768], P(('seq', 'shard'))
- second_shift_grad: float32 [768], P(('seq', 'shard'))
Inputs may be any that keep to these rules, and one draw needn't show every extreme that they name: `segments`: ids never fall along a sequence and start at 0; in at least one sequence one document begins within the first 512 tokens and ends within the last 512; the padding tokens form the sequence's last document, with id 2048 - 1. `live_mask`: each sequence ends with 1 to 256 padding tokens, marked 0; all others are 1.
All inputs are finite; a program needn't handle non-finite values.
Results may differ from a plain program's by a relative error of at most 0.02.
Values may be sent and summed in bfloat16 or wider, within the bound.
A program may use at most 128 MiB of HBM per device.

v0:
```python
import functools
import jax
import jax.numpy as jnp
from jax import lax
from jax.experimental import pallas as pl
from jax.experimental.pallas import tpu as pltpu
from jax.sharding import PartitionSpec as P

MESH = pl.DeviceIdType.MESH
ANY = pl.BlockSpec(memory_space=pl.ANY)
VMEM_LIMIT = 56 << 20
VM = pl.BlockSpec(memory_space=pltpu.VMEM)


class Place:
    def __init__(self):
        b = lax.axis_index("blk")
        s = lax.axis_index("seq")
        h = lax.axis_index("shard")
        x = h // 2
        c = h % 2
        self.b, self.s, self.h, self.x, self.c = b, s, h, x, c
        self.X = (b, s, (1 - x) * 2 + c)
        self.Y = (b, 1 - s, h)
        self.C = (b, s, x * 2 + 1 - c)
        self.L = (b - 1, s, h)
        self.R = (b + 1, s, h)
        self.me = s * 4 + h
        self.xi = s * 4 + (1 - x) * 2 + c
        self.yi = (1 - s) * 4 + h
        self.di = (1 - s) * 4 + (1 - x) * 2 + c

    def z(self, j):
        return (j, self.s, self.h)


def enter(p, nb, plane, line):
    bar = pltpu.get_barrier_semaphore()
    count = 0
    if plane:
        for peer in (p.X, p.Y, p.C):
            pl.semaphore_signal(bar, inc=1, device_id=peer, device_id_type=MESH)
        count = count + 3
    if line == "near":
        @pl.when(p.b > 0)
        def _():
            pl.semaphore_signal(bar, inc=1, device_id=p.L, device_id_type=MESH)

        @pl.when(p.b < nb - 1)
        def _():
            pl.semaphore_signal(bar, inc=1, device_id=p.R, device_id_type=MESH)
        count = count + jnp.where(p.b > 0, 1, 0) + jnp.where(p.b < nb - 1, 1, 0)
    if line == "all":
        for j in range(nb):
            @pl.when(p.b != j)
            def _():
                pl.semaphore_signal(bar, inc=1, device_id=p.z(j), device_id_type=MESH)
        count = count + nb - 1
    pl.semaphore_wait(bar, count)


def rcopy(src, dst, ss, rs, dev):
    return pltpu.make_async_remote_copy(
        src_ref=src, dst_ref=dst, send_sem=ss, recv_sem=rs, device_id=dev, device_id_type=MESH
    )


class LineGather:
    def __init__(self, p, nb, own, out, ssem, rsem):
        self.p, self.nb, self.own, self.out, self.ssem, self.rsem = p, nb, own, out, ssem, rsem

    def _copies(self, t):
        p, nb = self.p, self.nb
        rb = p.b - t
        lb = p.b + t
        src_r = self.own if t == 0 else self.out.at[jnp.maximum(rb, 0)]
        src_l = self.own if t == 0 else self.out.at[jnp.minimum(lb, nb - 1)]
        right = rcopy(src_r, self.out.at[jnp.maximum(rb, 0)], self.ssem.at[0, t], self.rsem.at[0, t], p.R)
        left = rcopy(src_l, self.out.at[jnp.minimum(lb, nb - 1)], self.ssem.at[1, t], self.rsem.at[1, t], p.L)
        return right, left, (rb >= 0) & (p.b < nb - 1), (lb <= nb - 1) & (p.b > 0)

    def start(self, t):
        right, left, cr, cl = self._copies(t)
        pl.when(cr)(right.start)
        pl.when(cl)(left.start)

    def wait_recv(self, t):
        p, nb = self.p, self.nb
        right, left, _, _ = self._copies(t)
        pl.when(p.b - 1 - t >= 0)(right.wait_recv)
        pl.when(p.b + 1 + t <= nb - 1)(left.wait_recv)

    def wait_send(self, t):
        right, left, cr, cl = self._copies(t)
        pl.when(cr)(right.wait_send)
        pl.when(cl)(left.wait_send)


class PlaneGather:
    def __init__(self, p, own, out, ssem, rsem, lsem):
        rows = own.shape[0]
        half = rows // 2

        def whole(i):
            return out.at[pl.ds(pl.multiple_of(i * rows, rows), rows)]

        def low(i):
            return out.at[pl.ds(pl.multiple_of(i * rows, rows), half)]

        def high(i):
            return out.at[pl.ds(pl.multiple_of(i * rows + half, half), half)]

        def send(k, src, dst, dev):
            return rcopy(src, dst, ssem.at[k], rsem.at[k], dev)

        self.x = send(0, own, whole(p.me), p.X)
        self.y = send(1, own, whole(p.me), p.Y)
        self.c = send(2, own, whole(p.me), p.C)
        self.local = pltpu.make_async_copy(own, whole(p.me), lsem)
        self.fx = send(3, high(p.yi), high(p.yi), p.X)
        self.fy = send(4, low(p.xi), low(p.xi), p.Y)
        self.cx = send(5, whole(p.xi), whole(p.xi), p.C)
        self.cy = send(6, whole(p.yi), whole(p.yi), p.C)
        self.cd0 = send(7, low(p.di), low(p.di), p.C)
        self.cd1 = send(8, high(p.di), high(p.di), p.C)

    def start(self):
        for k in (self.x, self.y, self.c, self.local):
            k.start()

    def forward(self):
        self.x.wait_recv()
        self.fy.start()
        self.cx.start()
        self.y.wait_recv()
        self.fx.start()
        self.cy.start()

    def diag(self):
        self.fy.wait_recv()
        self.cd0.start()
        self.fx.wait_recv()
        self.cd1.start()

    def finish(self):
        self.local.wait()
        for k in (self.c, self.cx, self.cy, self.cd0, self.cd1):
            k.wait_recv()

    def drain(self):
        for k in (self.x, self.y, self.c, self.fx, self.fy, self.cx, self.cy, self.cd0, self.cd1):
            k.wait_send()


def staged(count, steps, body):
    def once(i, _):
        for at, todo in steps.items():
            @pl.when(i == at)
            def _():
                for f in todo:
                    f()
        body(i)
        return 0
    lax.fori_loop(0, count, once, 0)


def turn(b, nb, i):
    far = (i + 1) // 2
    j = jnp.where(i % 2 == 1, b - far, b + far)
    return (j >= 0) & (j <= nb - 1), jnp.clip(j, 0, nb - 1)


def row_loop(rows, chunk, body):
    if rows == chunk:
        body(0)
    else:
        def step(i, _):
            body(pl.multiple_of(i * chunk, chunk))
            return 0
        lax.fori_loop(0, rows // chunk, step, 0)


class PlaneReduce:
    def __init__(self, p, nb, g, out, buf, stage, ss, rs, ls):
        self.p, self.nb = p, nb
        self.P, self.BX, self.BY, self.CX, self.CY, self.Z = buf
        self.O = out
        self.R, self.C = g.shape[-2:]
        self.dt = g.dtype
        self.ss, self.rs = ss, rs
        h = self.R // 2
        self.h = h
        lo, hi = pl.ds(0, h), pl.ds(h, h)
        self.chunk = 16 if self.C > 1024 else 48
        self.g = g
        self.stage = stage
        self.own = None if stage is None else pltpu.make_async_copy(g.at[:, :, p.c], stage, ls)
        self.cA = rcopy(g.at[:, :, 1 - p.c], self.P, ss.at[0], rs.at[0], p.C)
        self.cBX = rcopy(self.P.at[:, 1 - p.x, lo], self.BX, ss.at[1], rs.at[1], p.X)
        self.cBY = rcopy(self.P.at[1 - p.s, :, hi], self.BY, ss.at[2], rs.at[2], p.Y)
        self.cCX = rcopy(self.P.at[p.s, 1 - p.x, hi], self.CX, ss.at[3], rs.at[3], p.X)
        self.cCY = rcopy(self.P.at[1 - p.s, p.x, lo], self.CY, ss.at[4], rs.at[4], p.Y)
        self.F = self.P.at[p.s, p.x]

    def quarter(self, ref, j):
        R, C = self.R, self.C
        r, c = (j // 2) * (R // 2), (j % 2) * (C // 2)
        if not isinstance(j, int):
            r, c = pl.multiple_of(r, R // 2), pl.multiple_of(c, C // 2)
        return ref.at[pl.ds(r, R // 2), pl.ds(c, C // 2)]

    def a_start(self):
        self.cA.start()

    def own_start(self):
        self.own.start()

    def b_start(self):
        if self.own is not None:
            self.own.wait()
        self.cA.wait_recv()

        def block(i, _):
            s, x = i // 2, i % 2

            def body(r):
                rows = pl.ds(r, self.chunk)
                mine = self.g[s, x, self.p.c, rows] if self.stage is None else self.stage[s, x, rows]
                self.P[s, x, rows] = (
                    mine.astype(jnp.float32) + self.P[s, x, rows].astype(jnp.float32)
                ).astype(self.dt)
            row_loop(self.R, self.chunk, body)
            return 0
        lax.fori_loop(0, 4, block, 0)
        self.cBX.start()
        self.cBY.start()

    def _add(self, dst, src):
        chunk = min(self.chunk * 2, self.h)

        def body(r):
            rows = pl.ds(r, chunk)
            dst[rows] = (dst[rows].astype(jnp.float32) + src[rows].astype(jnp.float32)).astype(self.dt)
        row_loop(self.h, chunk if self.h % chunk == 0 else self.h, body)

    def c_start(self):
        p, h = self.p, self.h
        lo, hi = pl.ds(0, h), pl.ds(h, h)
        self.cBX.wait_recv()
        self._add(self.P.at[1 - p.s, p.x, lo], self.BX.at[1 - p.s])
        self.cCY.start()
        self.cBY.wait_recv()
        self._add(self.P.at[p.s, 1 - p.x, hi], self.BY.at[1 - p.x])
        self.cCX.start()
        self._add(self.P.at[p.s, p.x, lo], self.BX.at[p.s])
        self._add(self.P.at[p.s, p.x, hi], self.BY.at[p.x])


    def _right(self, j):
        return rcopy(self.quarter(self.F, j), self.Z.at[j], self.ss.at[5 + j], self.rs.at[5 + j], self.p.R)

    def _left(self, j, last):
        slot = self.nb if last else j
        k = 5 + self.nb + j
        return rcopy(self.quarter(self.F, j), self.Z.at[slot], self.ss.at[k], self.rs.at[k], self.p.L)

    def plane_end(self):
        h = self.h
        self.cCY.wait_recv()
        self._add(self.F.at[pl.ds(0, h)], self.CY)
        self.cCX.wait_recv()
        self._add(self.F.at[pl.ds(h, h)], self.CX)

    def hop(self, t):
        nb, p = self.nb, self.p
        if t == 0:
            self.plane_end()

        @pl.when(p.b == t)
        def _():
            for j in range(nb - 1, t, -1):
                if t > 0:
                    self._right(j).wait_recv()
                    self._add(self.quarter(self.F, j), self.Z.at[j])
                self._right(j).start()

        @pl.when(p.b == nb - 1 - t)
        def _():
            for j in range(nb - 1 - t):
                if t > 0:
                    self._left(j, False).wait_recv()
                    self._add(self.quarter(self.F, j), self.Z.at[j])
                self._left(j, j == nb - 2 - t).start()

    def _spread(self, t):
        p, nb = self.p, self.nb
        k = 5 + 2 * nb + 2 * t
        r, l = p.b - t, p.b + t
        qr = self.quarter(self.O, jnp.maximum(r, 0))
        ql = self.quarter(self.O, jnp.minimum(l, nb - 1))
        right = rcopy(qr, qr, self.ss.at[k], self.rs.at[k], p.R)
        left = rcopy(ql, ql, self.ss.at[k + 1], self.rs.at[k + 1], p.L)
        return right, left, (r >= 0) & (p.b < nb - 1), (l <= nb - 1) & (p.b > 0)

    def _spread_recv(self, t):
        right, left, _, _ = self._spread(t)
        p, nb = self.p, self.nb
        pl.when(p.b - 1 - t >= 0)(right.wait_recv)
        pl.when(p.b + 1 + t <= nb - 1)(left.wait_recv)

    def spread(self, t):
        p, nb = self.p, self.nb
        if t == 0:
            mine = self.quarter(self.F, p.b)
            for j in range(nb):
                @pl.when(p.b == j)
                def _():
                    if j > 0:
                        self._right(j).wait_recv()
                        self._add(mine, self.Z.at[j])
                    if j < nb - 1:
                        self._left(j, True).wait_recv()
                        self._add(mine, self.Z.at[nb])
            total = self.quarter(self.O, p.b)

            def body(r):
                rows = pl.ds(r, self.chunk)
                total[rows] = mine[rows]
            row_loop(self.h, self.chunk, body)
        else:
            self._spread_recv(t - 1)
        right, left, cr, cl = self._spread(t)
        pl.when(cr)(right.start)
        pl.when(cl)(left.start)

    def finish(self):
        self._spread_recv(self.nb - 2)

    def drain(self):
        nb, p = self.nb, self.p
        for k in (self.cA, self.cBX, self.cBY, self.cCX, self.cCY):
            k.wait_send()
        for t in range(nb - 1):
            @pl.when(p.b == t)
            def _():
                for j in range(nb - 1, t, -1):
                    self._right(j).wait_send()

            @pl.when(p.b == nb - 1 - t)
            def _():
                for j in range(nb - 1 - t):
                    self._left(j, j == nb - 2 - t).wait_send()
            right, left, cr, cl = self._spread(t)
            pl.when(cr)(right.wait_send)
            pl.when(cl)(left.wait_send)


def reduce_scratch(shape, dt, nb):
    R, C = shape
    h = R // 2
    return [
        pltpu.VMEM((2, 2, R, C), dt),
        pltpu.VMEM((2, h, C), dt),
        pltpu.VMEM((2, h, C), dt),
        pltpu.VMEM((h, C), dt),
        pltpu.VMEM((h, C), dt),
        pltpu.VMEM((nb + 1, h, C // 2), dt),
    ]


NBUF = 6


def reduce_sems(nb):
    return 5 + 2 * nb + 2 * (nb - 1)


class TableSum:
    def __init__(self, p, nb, t, bufs, line, ss, rs):
        self.p, self.nb, self.t, self.bufs, self.line = p, nb, t, bufs, line
        self.steps = [
            rcopy(t if i == 0 else bufs.at[i - 1], bufs.at[3 + i], ss.at[i], rs.at[i], dev)
            for i, dev in enumerate((p.C, p.X, p.Y))
        ]
        self.ss, self.rs = ss, rs

    def start(self):
        self.steps[0].start()

    def step(self, i):
        self.steps[i].wait_recv()
        self.bufs[i] = (self.t[...] if i == 0 else self.bufs[i - 1]) + self.bufs[3 + i]
        if i < 2:
            self.steps[i + 1].start()
        else:
            self.line[self.p.b] = self.bufs[2]
            for j in range(self.nb):
                pl.when(self.p.b != j)(self._z(j, self.p.b).start)

    def _z(self, j, slot):
        return rcopy(
            self.bufs.at[2], self.line.at[slot], self.ss.at[3 + j], self.rs.at[3 + slot], self.p.z(j)
        )

    def finish(self, out):
        for j in range(self.nb):
            pl.when(self.p.b != j)(self._z(j, j).wait_recv)
        total = self.line[0]
        for j in range(1, self.nb):
            total = total + self.line[j]
        out[...] = total

    def drain(self):
        for k in self.steps:
            k.wait_send()
        for j in range(self.nb):
            pl.when(self.p.b != j)(self._z(j, self.p.b).wait_send)


HEAD_DIM = 64
PAIR = 128
MASKED = -1e30
TILE = 512


def dot(a, b, ca, cb):
    return lax.dot_general(a, b, (((ca,), (cb,)), ((), ())), preferred_element_type=jnp.float32)


def left_lanes(shape):
    return lax.broadcasted_iota(jnp.int32, shape, 1) < HEAD_DIM


def one_head(pair, left, first):
    keep = left if first else jnp.logical_not(left)
    return jnp.where(keep, pair, jnp.zeros_like(pair))


def lane_groups(op, a):
    out = a[:, :PAIR]
    for g in range(1, a.shape[1] // PAIR):
        out = op(out, a[:, g * PAIR:(g + 1) * PAIR])
    return out


def attn_fwd_kernel(span, col_ref, row_ref, q_ref, k_ref, v_ref, o_ref, ob_ref, lse_ref, s_ref, m_ref, l_ref, acc_ref):
    rows = q_ref.shape[0]
    left = left_lanes((rows, PAIR))
    m_ref[...] = jnp.full_like(m_ref, MASKED)
    l_ref[...] = jnp.zeros_like(l_ref)
    acc_ref[...] = jnp.zeros_like(acc_ref)
    q = q_ref[...]
    heads = [one_head(q, left, i == 0) for i in range(2)]
    codes = col_ref[...]

    def score(t, _):
        at = pl.multiple_of(t * TILE, TILE)
        k = k_ref[pl.ds(at, TILE), :]
        mask = codes == row_ref[:, pl.ds(at, TILE)]
        for i in range(2):
            s = jnp.where(mask, dot(heads[i], k, 1, 1), MASKED)
            s_ref[i, t] = s
            m_ref[i] = jnp.maximum(m_ref[i], lane_groups(jnp.maximum, s))
        return 0

    lax.fori_loop(span[0], span[1], score, 0)
    tops = [jnp.max(m_ref[i], axis=1, keepdims=True) for i in range(2)]

    def mix(t, _):
        v = v_ref[pl.ds(pl.multiple_of(t * TILE, TILE), TILE), :]
        parts = []
        for i in range(2):
            p = jnp.exp(s_ref[i, t] - tops[i])
            l_ref[i] += lane_groups(jnp.add, p)
            parts.append(dot(p.astype(jnp.bfloat16), v, 1, 0))
        acc_ref[...] += jnp.where(left, parts[0], parts[1])
        return 0

    lax.fori_loop(span[0], span[1], mix, 0)
    sums = [jnp.sum(l_ref[i], axis=1, keepdims=True) for i in range(2)]
    total = jnp.where(left, sums[0], sums[1])
    o = acc_ref[...] / total
    o_ref[...] = o
    ob_ref[...] = o.astype(jnp.bfloat16)
    lse_ref[...] = jnp.where(left, tops[0], tops[1]) + jnp.log(total)


def attention(q, k_all, v_all, codes, own_codes, span):
    rows, width = q.shape
    total = k_all.shape[0]
    pairs = width // PAIR
    own = pl.BlockSpec((rows, PAIR), lambda h, s: (0, h))
    every = pl.BlockSpec((total, PAIR), lambda h, s: (0, h))
    return pl.pallas_call(
        attn_fwd_kernel,
        grid_spec=pltpu.PrefetchScalarGridSpec(
            num_scalar_prefetch=1,
            grid=(pairs,),
            in_specs=[
                pl.BlockSpec((rows, 1), lambda h, s: (0, 0)),
                pl.BlockSpec((1, total), lambda h, s: (0, 0)),
                own, every, every,
            ],
            out_specs=[own, own, own],
            scratch_shapes=[
                pltpu.VMEM((2, total // TILE, rows, TILE), jnp.float32),
                pltpu.VMEM((2, rows, PAIR), jnp.float32),
                pltpu.VMEM((2, rows, PAIR), jnp.float32),
                pltpu.VMEM((rows, PAIR), jnp.float32),
            ],
        ),
        out_shape=[
            jax.ShapeDtypeStruct((rows, width), jnp.float32),
            jax.ShapeDtypeStruct((rows, width), jnp.bfloat16),
            jax.ShapeDtypeStruct((rows, width), jnp.float32),
        ],
        compiler_params=pltpu.CompilerParams(vmem_limit_bytes=48 << 20),
        name="attention",
    )(span, own_codes.reshape(rows, 1), codes.reshape(1, total), q, k_all, v_all)


def stats_kernel(g_ref, o_ref, lse_ref, out_ref, delta_ref):
    rows = g_ref.shape[0]
    left = left_lanes((rows, PAIR))
    t = g_ref[...].astype(jnp.float32) * o_ref[...]
    d0 = jnp.sum(jnp.where(left, t, 0.0), axis=1, keepdims=True)
    d1 = jnp.sum(jnp.where(left, 0.0, t), axis=1, keepdims=True)
    delta_ref[...] = jnp.where(left, d0, d1)
    lane = lax.broadcasted_iota(jnp.int32, (rows, PAIR), 1)
    lse = lse_ref[...]
    packed = jnp.where(lane == 0, lse[:, :1], jnp.where(lane == 1, lse[:, HEAD_DIM:HEAD_DIM + 1], jnp.where(lane == 2, d0, d1)))
    out_ref[0] = packed.T[:8]


def row_stats(grad, o, lse):
    rows, width = grad.shape
    pairs = width // PAIR
    own = pl.BlockSpec((rows, PAIR), lambda h: (0, h))
    return pl.pallas_call(
        stats_kernel,
        grid=(pairs,),
        in_specs=[own, own, own],
        out_specs=[pl.BlockSpec((1, 8, rows), lambda h: (h, 0, 0)), own],
        out_shape=[
            jax.ShapeDtypeStruct((pairs, 8, rows), jnp.float32),
            jax.ShapeDtypeStruct((rows, width), jnp.float32),
        ],
        name="row_stats",
    )(grad, o, lse)


def attn_bwd_kernel(span, col_ref, row_ref, q_ref, k_ref, v_ref, g_ref, lse_ref, delta_ref,
                    qa_ref, ka_ref, va_ref, ga_ref, st_ref, dq_ref, dk_ref, dv_ref):
    rows = q_ref.shape[0]
    left = left_lanes((rows, PAIR))
    dq_ref[...] = jnp.zeros_like(dq_ref)
    dk_ref[...] = jnp.zeros_like(dk_ref)
    dv_ref[...] = jnp.zeros_like(dv_ref)
    codes = col_ref[...]
    qs = [one_head(q_ref[...], left, i == 0) for i in range(2)]
    ks = [one_head(k_ref[...], left, i == 0) for i in range(2)]
    vs = [one_head(v_ref[...], left, i == 0) for i in range(2)]
    gs = [one_head(g_ref[...], left, i == 0) for i in range(2)]
    lses = [lse_ref[:, i * HEAD_DIM:i * HEAD_DIM + 1] for i in range(2)]
    deltas = [delta_ref[:, i * HEAD_DIM:i * HEAD_DIM + 1] for i in range(2)]

    def step(t, _):
        at = pl.multiple_of(t * TILE, TILE)
        tile = pl.ds(at, TILE)
        mask = codes == row_ref[:, tile]
        k, v, q, g = ka_ref[tile, :], va_ref[tile, :], qa_ref[tile, :], ga_ref[tile, :]
        dqs, dks, dvs = [], [], []
        for i in range(2):
            s = jnp.where(mask, dot(qs[i], k, 1, 1), MASKED)
            p = jnp.exp(s - lses[i])
            dp = dot(gs[i], v, 1, 1)
            ds = (p * (dp - deltas[i])).astype(jnp.bfloat16)
            dqs.append(dot(ds, k, 1, 0))
            st = jnp.where(mask, dot(ks[i], q, 1, 1), MASKED)
            pt = jnp.exp(st - st_ref[0, i:i + 1, tile])
            dvs.append(dot(pt.astype(jnp.bfloat16), g, 1, 0))
            dpt = dot(vs[i], g, 1, 1)
            dst = (pt * (dpt - st_ref[0, 2 + i:3 + i, tile])).astype(jnp.bfloat16)
            dks.append(dot(dst, q, 1, 0))
        dq_ref[...] += jnp.where(left, dqs[0], dqs[1])
        dk_ref[...] += jnp.where(left, dks[0], dks[1])
        dv_ref[...] += jnp.where(left, dvs[0], dvs[1])
        return 0

    lax.fori_loop(span[0], span[1], step, 0)


def attention_grad(q, k, v, g, lse, delta, q_all, k_all, v_all, g_all, stats, codes, own_codes, span):
    rows, width = q.shape
    total = k_all.shape[0]
    pairs = width // PAIR
    own = pl.BlockSpec((rows, PAIR), lambda h, s: (0, h))
    every = pl.BlockSpec((total, PAIR), lambda h, s: (0, h))
    return pl.pallas_call(
        attn_bwd_kernel,
        grid_spec=pltpu.PrefetchScalarGridSpec(
            num_scalar_prefetch=1,
            grid=(pairs,),
            in_specs=[
                pl.BlockSpec((rows, 1), lambda h, s: (0, 0)),
                pl.BlockSpec((1, total), lambda h, s: (0, 0)),
                own, own, own, own, own, own, every, every, every, every,
                pl.BlockSpec((1, 8, total), lambda h, s: (h, 0, 0)),
            ],
            out_specs=[own, own, own],
        ),
        out_shape=[
            jax.ShapeDtypeStruct((rows, width), jnp.float32),
            jax.ShapeDtypeStruct((rows, width), jnp.float32),
            jax.ShapeDtypeStruct((rows, width), jnp.float32),
        ],
        compiler_params=pltpu.CompilerParams(vmem_limit_bytes=48 << 20),
        name="attention_grad",
    )(span, own_codes.reshape(rows, 1), codes.reshape(1, total), q, k, v, g, lse, delta, q_all, k_all, v_all, g_all, stats)


VEC_ROWS = 8


def forward_kernel(nb, *refs):
    x_ref, codes, rows = refs[:3]
    shards_in = refs[3:9]
    vecs_in = refs[9:18]
    wq_o, wk_o, wv_o, wo_o, wup_o, wdn_o = refs[18:24]
    q_o, k_o, v_o = refs[24:27]
    o_ref, ob_ref, lse_ref, vec_ref, bup_ref = refs[27:32]
    rest = refs[32:]
    x_all, wq, wk, wv, pack, packs, q, k, v, m_ref, l_ref = rest[:11]
    zs, zr, gs, gr, gl, ws, es = rest[11:]
    n, width = x_ref.shape
    pairs = width // PAIR
    p = Place()
    own = pltpu.make_async_copy(x_ref, x_all.at[p.b], ws.at[3])
    own.start()
    pack[...] = jnp.zeros_like(pack)
    for i in range(VEC_ROWS):
        pack[i:i + 1, :vecs_in[i].shape[1]] = vecs_in[i][...].astype(jnp.float32)
    for i in range(vecs_in[8].shape[1] // PAIR):
        pack[VEC_ROWS + i:VEC_ROWS + i + 1, :] = vecs_in[8][:, i * PAIR:(i + 1) * PAIR].astype(jnp.float32)
    enter(p, nb, True, "near")
    line = LineGather(p, nb, x_ref, x_all, zs, zr)
    targets = (packs, wq, wk, wv, wo_o, wup_o, wdn_o)
    sources = (pack,) + tuple(shards_in)
    g = [PlaneGather(p, sources[i], targets[i], gs.at[i], gr.at[i], gl.at[i]) for i in range(7)]
    line.start(0)
    for c in g[:5]:
        c.start()
    for c in g[:4]:
        c.forward()
    g[5].start()
    g[6].start()
    line.wait_recv(0)
    line.start(1)
    for c in g[:4]:
        c.diag()
    for c in g[:4]:
        c.finish()
    own.wait()
    keep = [
        pltpu.make_async_copy(a, b, ws.at[i]) for i, (a, b) in enumerate(((wq, wq_o), (wk, wk_o), (wv, wv_o)))
    ]
    for c in keep:
        c.start()

    piece = width // 8
    r = lax.broadcasted_iota(jnp.int32, (PAIR, width), 0)
    c = lax.broadcasted_iota(jnp.int32, (PAIR, width), 1)
    total = jnp.zeros((2 * VEC_ROWS, width), jnp.float32)
    for i in range(8):
        pick = ((c == r + i * piece) & (r < piece)).astype(jnp.bfloat16)
        total += dot(packs[2 * VEC_ROWS * i:2 * VEC_ROWS * (i + 1), :].astype(jnp.bfloat16), pick, 1, 0)
    vec_ref[...] = total[:VEC_ROWS]
    up_piece = bup_ref.shape[1] // 8
    for i in range(8):
        for t in range(up_piece // PAIR):
            at = i * up_piece + t * PAIR
            row = 2 * VEC_ROWS * i + VEC_ROWS + t
            bup_ref[:, at:at + PAIR] = packs[row:row + 1, :]

    scale = HEAD_DIM ** (-0.5)
    step = 256

    def outs(j, e):
        return [
            pltpu.make_async_copy(a.at[j], b.at[j], es.at[i, e])
            for i, (a, b) in enumerate(((q, q_o), (k, k_o), (v, v_o)))
        ]

    def project(j):
        def columns(t, _):
            at = pl.ds(pl.multiple_of(t * step, step), step)
            xs = x_all[j]
            q[j, :, at] = ((dot(xs, wq[:, at], 1, 0) + vec_ref[0:1, at]) * scale).astype(jnp.bfloat16)
            k[j, :, at] = dot(xs, wk[:, at], 1, 0).astype(jnp.bfloat16)
            v[j, :, at] = (dot(xs, wv[:, at], 1, 0) + vec_ref[1:2, at]).astype(jnp.bfloat16)
            return 0
        lax.fori_loop(0, width // step, columns, 0, unroll=True)

    def attend(j):
        def pair(h, _):
            left = left_lanes((n, PAIR))
            lanes = pl.ds(pl.multiple_of(h * PAIR, PAIR), PAIR)
            mask = codes[...] == rows[j]
            qs, ks, vs = q[p.b, :, lanes], k[j, :, lanes], v[j, :, lanes]
            parts, alphas = [], []
            for i in range(2):
                s = jnp.where(mask, dot(one_head(qs, left, i == 0), ks, 1, 1), MASKED)
                top = jnp.max(lane_groups(jnp.maximum, s), axis=1, keepdims=True)
                old = m_ref[2 * h + i]
                new = jnp.maximum(old, top)
                alpha = jnp.exp(old - new)
                e = jnp.exp(s - jnp.concatenate([new] * (n // PAIR), axis=1))
                m_ref[2 * h + i] = new
                l_ref[2 * h + i] = l_ref[2 * h + i] * alpha + lane_groups(jnp.add, e)
                alphas.append(alpha)
                parts.append(dot(e.astype(jnp.bfloat16), vs, 1, 0))
            got = jnp.where(left, parts[0], parts[1])
            o_ref[:, lanes] = o_ref[:, lanes] * jnp.where(left, alphas[0], alphas[1]) + got
            return 0
        lax.fori_loop(0, pairs, pair, 0, unroll=2)

    def block(i):
        ok, j = turn(p.b, nb, i)

        @pl.when(ok)
        def _():
            project(j)
            for c in outs(j, i):
                c.start()
            attend(j)

    def hop(t, last=False):
        line.wait_recv(t)
        if not last:
            line.start(t + 1)

    m_ref[...] = jnp.full_like(m_ref, MASKED)
    l_ref[...] = jnp.zeros_like(l_ref)
    o_ref[...] = jnp.zeros_like(o_ref)
    staged(
        2 * nb - 1,
        {
            1: [g[4].forward, g[5].forward],
            2: [lambda: hop(1)],
            3: [g[6].forward, g[4].diag],
            5: [g[5].diag, g[6].diag, lambda: hop(2, True)],
        },
        block,
    )

    def close(h, _):
        left = left_lanes((n, PAIR))
        lanes = pl.ds(pl.multiple_of(h * PAIR, PAIR), PAIR)
        sums = [jnp.sum(l_ref[2 * h + i], axis=1, keepdims=True) for i in range(2)]
        mass = jnp.where(left, sums[0], sums[1])
        out = o_ref[:, lanes] / mass
        o_ref[:, lanes] = out
        ob_ref[:, lanes] = out.astype(jnp.bfloat16)
        lse_ref[:, lanes] = jnp.where(left, m_ref[2 * h], m_ref[2 * h + 1]) + jnp.log(mass)
        return 0
    lax.fori_loop(0, pairs, close, 0)
    for c in g[4:]:
        c.finish()
    for c in keep:
        c.wait()
    for i in range(2 * nb - 1):
        ok, j = turn(p.b, nb, i)

        @pl.when(ok)
        def _():
            for c in outs(j, i):
                c.wait()
    for t in range(nb - 1):
        line.wait_send(t)
    for c in g:
        c.drain()


def forward(x, codes, own_codes, weights, vecs, nb):
    n, width = x.shape
    hidden = weights[4].shape[1]
    bf, f32 = jnp.bfloat16, jnp.float32
    every = jax.ShapeDtypeStruct((nb, n, width), bf)
    block = jax.ShapeDtypeStruct((n, width), f32)
    mats = [jax.ShapeDtypeStruct((8 * w.shape[0], w.shape[1]), w.dtype) for w in weights]
    dma = pltpu.SemaphoreType.DMA
    return pl.pallas_call(
        functools.partial(forward_kernel, nb),
        out_shape=(
            *mats, every, every, every, block, jax.ShapeDtypeStruct((n, width), bf), block,
            jax.ShapeDtypeStruct((VEC_ROWS, width), f32), jax.ShapeDtypeStruct((1, hidden), f32),
        ),
        in_specs=[VM] * 18,
        out_specs=(ANY,) * 9 + (VM,) * 5,
        scratch_shapes=[
            pltpu.VMEM((nb, n, width), bf),
            pltpu.VMEM((width, width), bf), pltpu.VMEM((width, width), bf), pltpu.VMEM((width, width), bf),
            pltpu.VMEM((2 * VEC_ROWS, PAIR), f32), pltpu.VMEM((16 * VEC_ROWS, PAIR), f32),
            pltpu.VMEM((nb, n, width), bf), pltpu.VMEM((nb, n, width), bf), pltpu.VMEM((nb, n, width), bf),
            pltpu.VMEM((width // HEAD_DIM, n, PAIR), f32), pltpu.VMEM((width // HEAD_DIM, n, PAIR), f32),
            dma((2, nb - 1)), dma((2, nb - 1)), dma((7, 9)), dma((7, 9)), dma((7,)), dma((4,)), dma((3, 2 * nb)),
        ],
        compiler_params=pltpu.CompilerParams(
            collective_id=1, has_side_effects=True, vmem_limit_bytes=60 << 20
        ),
        name="forward",
    )(
        x, own_codes.reshape(n, 1), codes.reshape(nb, 1, n), *weights, *[v.reshape(1, -1) for v in vecs]
    )


ROOT_HALF = 0.7071067811865476
ROOT_TWO_PI = 0.3989422804014327
CHUNK = 768
PART = 256


def erf_parts(x):
    x = jnp.clip(x, -3.832506856900711, 3.832506856900711)
    y = x * x
    top = jnp.full_like(y, 0.00022905065861350646)
    for a in (0.0034082910107109506, 0.050955695062380861, 0.18520832239976145, 1.128379143519084):
        top = top * y + a
    low = jnp.full_like(y, -1.1791602954361697e-7)
    for a in (
        0.000023547966471313185, 0.0010179625278914885, 0.014070470171167667,
        0.11098505178285362, 0.49746925110067538, 1.0,
    ):
        low = low * y + a
    return x * top / low


def middle_kernel(
    att_ref, x_ref, cot_ref, o_ref, lse_ref, vec_ref, bup_ref, wo_hbm, wup_hbm, wdn_hbm,
    out_ref, rest_ref, do_ref, stats_ref, delta_ref, table_ref, gdn_hbm, gup_hbm, gwo_ref,
    wo, wup, wdn, u_ref, slope_ref, y_ref, dh_ref, low_ref, gdn, gup, sems, osems,
):
    n, width = x_ref.shape
    hidden = wup.shape[1]
    chunks = hidden // CHUNK
    f32, bf = jnp.float32, jnp.bfloat16
    loads = [
        pltpu.make_async_copy(a, b, sems.at[i])
        for i, (a, b) in enumerate(((wo_hbm, wo), (wup_hbm, wup), (wdn_hbm, wdn)))
    ]
    for c in loads:
        c.start()
    table_ref[...] = jnp.zeros_like(table_ref)

    def vec(i):
        return vec_ref[i:i + 1, :]

    def mean(a):
        return jnp.sum(a, axis=1, keepdims=True) * (1.0 / width)

    def centred(h):
        c = h - mean(h)
        inv = lax.rsqrt(mean(c * c) + EPSILON)
        return c * inv, inv

    def pull(grad, hat, inv, gain):
        d = grad * gain
        return inv * (d - mean(d) - hat * mean(d * hat))

    def column_sum(a):
        return jnp.sum(a, axis=0, keepdims=True)

    blocks = 4
    m = n // blocks

    def rows_of(i):
        return pl.ds(pl.multiple_of(i * m, m), m)

    loads[0].wait()

    def first(i, _):
        r = rows_of(i)
        h = x_ref[r, :].astype(f32) + dot(att_ref[r, :], wo[...], 1, 0) + vec(2)
        hat, _ = centred(h)
        y = hat * vec(3) + vec(4)
        rest_ref[r, :] = h
        dh_ref[r, :] = y + vec(5)
        low_ref[r, :] = y.astype(bf)
        return 0
    lax.fori_loop(0, blocks, first, 0)
    for c in loads[1:]:
        c.wait()

    def up(t, _):
        total = dh_ref[...]
        for s in range(CHUNK // PART):
            at = pl.ds(pl.multiple_of(t * CHUNK + s * PART, PART), PART)
            z = dot(low_ref[...], wup[:, at], 1, 0) + bup_ref[:, at]
            cdf = 0.5 + 0.5 * erf_parts(z * ROOT_HALF)
            low = (z * cdf).astype(bf)
            u_ref[:, at] = low
            slope_ref[:, at] = cdf + z * (jnp.exp(-0.5 * z * z) * ROOT_TWO_PI)
            total = total + dot(low, wdn[at, :], 1, 0)
        dh_ref[...] = total
        return 0
    lax.fori_loop(0, chunks, up, 0)

    def second(i, _):
        r = rows_of(i)
        hat, inv = centred(dh_ref[r, :])
        out_ref[r, :] = (hat * vec(6) + vec(7)).astype(bf)
        g = cot_ref[r, :].astype(f32)
        table_ref[6:7, :] += column_sum(g * hat)
        table_ref[7:8, :] += column_sum(g)
        dh = pull(g, hat, inv, vec(6))
        table_ref[5:6, :] += column_sum(dh)
        dh_ref[r, :] = dh
        y_ref[r, :] = dh.astype(bf)
        return 0
    lax.fori_loop(0, blocks, second, 0)

    def down(t, _):
        at = pl.ds(pl.multiple_of(t * CHUNK, CHUNK), CHUNK)
        parts = []
        total = dh_ref[...]
        for s in range(CHUNK // PART):
            cols = pl.ds(pl.multiple_of(t * CHUNK + s * PART, PART), PART)
            dz = dot(y_ref[...], wdn[cols, :], 1, 1) * slope_ref[:, cols]
            table_ref[pl.ds(8 + t, 1), s * PART:(s + 1) * PART] = column_sum(dz)
            c = dz.astype(bf)
            parts.append(c)
            total = total + dot(c, wup[:, cols], 1, 1)
            gdn[cols, :] = dot(u_ref[:, cols], y_ref[...], 0, 0).astype(bf)
        dh_ref[...] = total
        c = jnp.concatenate(parts, axis=1)
        r = width // 8
        for i in range(2):
            half = width // 2
            g = dot(low_ref[:, i * half:(i + 1) * half], c, 0, 0).astype(bf)
            for k in range(4):
                gup[4 * i + k, t] = g[k * r:(k + 1) * r]
        pltpu.make_async_copy(gdn.at[at], gdn_hbm.at[at], osems.at[0, t]).start()
        pltpu.make_async_copy(gup.at[:, t], gup_hbm.at[:, t], osems.at[1, t]).start()
        return 0
    lax.fori_loop(0, chunks, down, 0)

    def third(i, _):
        r = rows_of(i)
        hat, inv = centred(rest_ref[r, :])
        g = dh_ref[r, :]
        table_ref[3:4, :] += column_sum(g * hat)
        table_ref[4:5, :] += column_sum(g)
        dh = pull(g, hat, inv, vec(3))
        table_ref[2:3, :] += column_sum(dh)
        rest_ref[r, :] = dh
        low = dh.astype(bf)
        low_ref[r, :] = low
        do_ref[r, :] = dot(low, wo[...], 1, 1).astype(bf)
        return 0
    lax.fori_loop(0, blocks, third, 0)

    def heads(h, _):
        lanes = pl.ds(pl.multiple_of(h * PAIR, PAIR), PAIR)
        left = left_lanes((n, PAIR))
        t = do_ref[:, lanes].astype(f32) * o_ref[:, lanes]
        d0 = jnp.sum(jnp.where(left, t, 0.0), axis=1, keepdims=True)
        d1 = jnp.sum(jnp.where(left, 0.0, t), axis=1, keepdims=True)
        delta_ref[:, lanes] = jnp.where(left, d0, d1)
        lane = lax.broadcasted_iota(jnp.int32, (n, PAIR), 1)
        lse = lse_ref[:, lanes]
        packed = jnp.where(lane == 0, lse[:, :1], jnp.where(
            lane == 1, lse[:, HEAD_DIM:HEAD_DIM + 1], jnp.where(lane == 2, d0, d1)))
        stats_ref[h] = packed.T[:8]
        gwo_ref[lanes, :] = dot(att_ref[:, lanes], low_ref[...], 0, 0).astype(bf)
        return 0
    lax.fori_loop(0, width // PAIR, heads, 0)
    for t in range(chunks):
        at = pl.ds(t * CHUNK, CHUNK)
        pltpu.make_async_copy(gdn.at[at], gdn_hbm.at[at], osems.at[0, t]).wait()
        pltpu.make_async_copy(gup.at[:, t], gup_hbm.at[:, t], osems.at[1, t]).wait()


def middle(att, x, cot, o, lse, vecs, bup, wo, wup, wdn):
    n, width = x.shape
    hidden = wup.shape[1]
    chunks = hidden // CHUNK
    bf, f32 = jnp.bfloat16, jnp.float32
    S = jax.ShapeDtypeStruct
    dma = pltpu.SemaphoreType.DMA
    return pl.pallas_call(
        middle_kernel,
        out_shape=(
            S((n, width), bf), S((n, width), f32), S((n, width), bf), S((width // PAIR, 8, n), f32),
            S((n, width), f32), S((16, width), f32), S((hidden, width), bf),
            S((8, chunks, width // 8, CHUNK), bf), S((width, width), bf),
        ),
        in_specs=[VM] * 7 + [ANY] * 3,
        out_specs=(VM,) * 6 + (ANY, ANY, VM),
        scratch_shapes=[
            pltpu.VMEM((width, width), bf), pltpu.VMEM((width, hidden), bf), pltpu.VMEM((hidden, width), bf),
            pltpu.VMEM((n, hidden), bf), pltpu.VMEM((n, hidden), f32), pltpu.VMEM((n, width), bf),
            pltpu.VMEM((n, width), f32), pltpu.VMEM((n, width), bf),
            pltpu.VMEM((hidden, width), bf), pltpu.VMEM((8, chunks, width // 8, CHUNK), bf),
            dma((3,)), dma((2, chunks)),
        ],
        compiler_params=pltpu.CompilerParams(vmem_limit_bytes=60 << 20),
        name="middle",
    )(att, x, cot, o, lse, vecs, bup, wo, wup, wdn)


class AttentionGrad:
    def __init__(self, codes, rows, q, k, v, g, lse, delta, stats, own, dq, dk, dv):
        self.codes, self.rows = codes, rows
        self.q, self.k, self.v, self.g = q, k, v, g
        self.lse, self.delta, self.stats = lse, delta, stats
        self.own = own
        self.dq, self.dk, self.dv = dq, dk, dv
        self.n = dq.shape[0]
        self.pairs = dq.shape[1] // PAIR

    def queries(self, j):
        own = self.own

        def pair(h, _):
            left = left_lanes((self.n, PAIR))
            lanes = pl.ds(pl.multiple_of(h * PAIR, PAIR), PAIR)
            mask = self.codes[...] == self.rows[j]
            q, g = self.q[own, :, lanes], self.g[own, :, lanes]
            k, v = self.k[j, :, lanes], self.v[j, :, lanes]
            lse, delta = self.lse[:, lanes], self.delta[:, lanes]
            parts = []
            for i in range(2):
                at = slice(i * HEAD_DIM, i * HEAD_DIM + 1)
                s = jnp.where(mask, dot(one_head(q, left, i == 0), k, 1, 1), MASKED)
                p = jnp.exp(s - lse[:, at])
                dp = dot(one_head(g, left, i == 0), v, 1, 1)
                ds = (p * (dp - delta[:, at])).astype(jnp.bfloat16)
                parts.append(dot(ds, k, 1, 0))
            self.dq[:, lanes] += jnp.where(left, parts[0], parts[1])
            return 0

        lax.fori_loop(0, self.pairs, pair, 0, unroll=2)

    def keys(self, j):
        own = self.own

        def pair(h, _):
            left = left_lanes((self.n, PAIR))
            lanes = pl.ds(pl.multiple_of(h * PAIR, PAIR), PAIR)
            mask = self.codes[...] == self.rows[j]
            k, v = self.k[own, :, lanes], self.v[own, :, lanes]
            q, g = self.q[j, :, lanes], self.g[j, :, lanes]
            dks, dvs = [], []
            for i in range(2):
                st = jnp.where(mask, dot(one_head(k, left, i == 0), q, 1, 1), MASKED)
                pt = jnp.exp(st - self.stats[j, h, i:i + 1])
                dvs.append(dot(pt.astype(jnp.bfloat16), g, 1, 0))
                dpt = dot(one_head(v, left, i == 0), g, 1, 1)
                dst = (pt * (dpt - self.stats[j, h, 2 + i:3 + i])).astype(jnp.bfloat16)
                dks.append(dot(dst, q, 1, 0))
            self.dk[:, lanes] += jnp.where(left, dks[0], dks[1])
            self.dv[:, lanes] += jnp.where(left, dvs[0], dvs[1])
            return 0

        lax.fori_loop(0, self.pairs, pair, 0, unroll=2)


TABLE = 16


def backward_kernel(nb, *refs):
    codes, rows, g_own, st_own, lse, delta, x_ref, rest_ref, table = refs[:9]
    q_hbm, k_hbm, v_hbm, wq_hbm, wk_hbm, wv_hbm = refs[9:15]
    early = refs[15:18]
    token_ref, table_out = refs[18:20]
    outs = refs[20:26]
    rest = refs[26:]
    q, k, v, g, stats, dq, dk, dv, wq, wk, wv, gw, stage_a, stage_b, tab, tsum, tline = rest[:17]
    bufs = rest[17:17 + 6 * NBUF]
    zs, zr, ls, ss, rs, rls, ts, tr = rest[17 + 6 * NBUF:]
    n, width = g_own.shape
    p = Place()
    loads = [
        pltpu.make_async_copy(a, b, ls.at[i])
        for i, (a, b) in enumerate((
            (k_hbm, k), (v_hbm, v), (q_hbm, q), (g_own, g.at[p.b]), (st_own, stats.at[p.b]),
            (wq_hbm, wq), (wk_hbm, wk), (wv_hbm, wv),
        ))
    ]
    for c in loads:
        c.start()
    enter(p, nb, True, "all")
    lines = [
        LineGather(p, nb, g_own, g, zs.at[0], zr.at[0]),
        LineGather(p, nb, st_own, stats, zs.at[1], zr.at[1]),
    ]
    sources = tuple(early) + tuple(gw.at[i] for i in range(3))
    stages = (stage_a, stage_a, stage_b, None, None, None)
    dn, up, wo, gq, gk, gv = [
        PlaneReduce(
            p, nb, sources[i], outs[i], bufs[NBUF * i:NBUF * (i + 1)],
            None if stages[i] is None else stages[i].reshape(sources[i].shape[:2] + sources[i].shape[3:]),
            ss.at[i], rs.at[i], rls.at[i],
        )
        for i in range(6)
    ]
    vec = TableSum(p, nb, tab, tsum, tline, ts, tr)
    for c in lines:
        c.start(0)
    for c in (dn, up, wo):
        c.a_start()
    dn.own_start()
    wo.own_start()
    work = AttentionGrad(codes, rows, q, k, v, g, lse, delta, stats, p.b, dq, dk, dv)
    for c in (dq, dk, dv):
        c[...] = jnp.zeros_like(c)
    for i in (0, 1, 2, 3):
        loads[i].wait()

    low = k
    def slot(i):
        return (p.b + 1 + i) % nb

    def settle(i, src, scale, row):
        value = src[...] if scale is None else src[...] * scale
        if row is not None:
            tab[row:row + 1, :] = jnp.sum(value, axis=0, keepdims=True)
        low[slot(i)] = value.astype(jnp.bfloat16)

    def weight_grad(i):
        half = width // 2
        for m in range(2):
            part = dot(x_ref[:, m * half:(m + 1) * half], low[slot(i)], 0, 0).astype(jnp.bfloat16)
            r = gw.shape[-2]
            for a in range(2):
                for b in range(2):
                    at = (2 * a + b) * r
                    gw[i, m, a, b] = part[at:at + r]

    def hop(t, last=False):
        for c in lines:
            c.wait_recv(t)
            if not last:
                c.start(t + 1)

    staged(
        nb,
        {
            1: [dn.b_start, up.own_start],
            2: [up.b_start, wo.b_start, lambda: hop(0)],
            3: [dn.c_start],
        },
        lambda i: work.queries((p.b + i) % nb),
    )
    for i in (4, 5, 6, 7):
        loads[i].wait()
    tab[...] = table[...]
    settle(0, dq, HEAD_DIM ** (-0.5), 0)
    weight_grad(0)
    gq.a_start()
    hop(1)
    up.c_start()

    def keys(i):
        ok, j = turn(p.b, nb, i)
        pl.when(ok)(lambda: work.keys(j))

    staged(
        2 * nb - 1,
        {
            1: [gq.b_start, wo.c_start],
            2: [lambda: dn.hop(0)],
            3: [lambda: up.hop(0), lambda: wo.hop(0), gq.c_start, lambda: dn.hop(1)],
            5: [lambda: up.hop(1), lambda: wo.hop(1), lambda: dn.hop(2), lambda: hop(2, True)],
        },
        keys,
    )
    settle(1, dk, None, None)
    settle(2, dv, None, 1)
    vec.start()
    weight_grad(1)
    gk.a_start()
    weight_grad(2)
    gv.a_start()
    up.hop(2)
    wo.hop(2)
    dn.spread(0)
    vec.step(0)
    gk.b_start()
    gv.b_start()
    gq.hop(0)
    vec.step(1)

    part = 256

    def columns(t, _):
        at = pl.ds(pl.multiple_of(t * part, part), part)
        total = rest_ref[:, at]
        for i, w in enumerate((wq, wk, wv)):
            total = total + dot(low[slot(i)], w[at, :], 1, 1)
        token_ref[:, at] = total.astype(jnp.bfloat16)
        return 0
    lax.fori_loop(0, width // part, columns, 0)

    up.spread(0)
    wo.spread(0)
    dn.spread(1)
    vec.step(2)
    gk.c_start()
    gv.c_start()
    gq.hop(1)
    up.spread(1)
    wo.spread(1)
    dn.spread(2)
    gq.hop(2)
    gk.hop(0)
    gv.hop(0)
    gq.spread(0)
    gk.hop(1)
    gv.hop(1)
    up.spread(2)
    wo.spread(2)
    gk.hop(2)
    gv.hop(2)
    gq.spread(1)
    gk.spread(0)
    gv.spread(0)
    gq.spread(2)
    gk.spread(1)
    gv.spread(1)
    gk.spread(2)
    gv.spread(2)
    vec.finish(table_out)
    every = (dn, up, wo, gq, gk, gv)
    for c in every:
        c.finish()
    for t in range(nb - 1):
        for c in lines:
            c.wait_send(t)
    for c in every:
        c.drain()
    vec.drain()


def backward(codes, own_codes, do, stats, lse, delta, x, rest, table, q_all, k_all, v_all, weights, early, nb):
    n, width = do.shape
    bf, f32 = jnp.bfloat16, jnp.float32
    late = jax.ShapeDtypeStruct((2, 2, 2, width // 8, width), bf)
    kinds = list(early) + [late] * 3
    scratch = []
    for g in kinds:
        scratch += reduce_scratch(g.shape[-2:], bf, nb)
    ns = reduce_sems(nb)
    every = pltpu.VMEM((nb, n, width), bf)
    total = pltpu.VMEM((n, width), f32)
    square = pltpu.VMEM((width, width), bf)
    dma = pltpu.SemaphoreType.DMA
    big, small = early[0].shape, early[2].shape
    return pl.pallas_call(
        functools.partial(backward_kernel, nb),
        out_shape=(
            jax.ShapeDtypeStruct((n, width), bf), jax.ShapeDtypeStruct((TABLE, width), f32),
            *[jax.ShapeDtypeStruct(g.shape[-2:], bf) for g in kinds],
        ),
        in_specs=[VM] * 9 + [ANY] * 9,
        out_specs=(VM,) * 8,
        scratch_shapes=[
            every, every, every, every, pltpu.VMEM((nb,) + stats.shape, f32), total, total, total,
            square, square, square, pltpu.VMEM((3,) + late.shape, bf),
            pltpu.VMEM(big[:2] + big[3:], bf), pltpu.VMEM(small[:2] + small[3:], bf),
            pltpu.VMEM((TABLE, width), f32), pltpu.VMEM((6, TABLE, width), f32), pltpu.VMEM((nb, TABLE, width), f32),
        ] + scratch + [
            dma((2, 2, nb - 1)), dma((2, 2, nb - 1)), dma((8,)), dma((6, ns)), dma((6, ns)), dma((3,)),
            dma((3 + nb,)), dma((3 + nb,)),
        ],
        compiler_params=pltpu.CompilerParams(
            collective_id=4, has_side_effects=True, vmem_limit_bytes=63 << 20
        ),
        name="backward",
    )(
        own_codes.reshape(n, 1), codes.reshape(nb, 1, n), do, stats, lse, delta, x, rest, table,
        q_all, k_all, v_all, *weights, *early,
    )


def finish_kernel(dn, up, wo, wq, wk, wv, table, token, *outs):
    f32 = jnp.float32
    outs[15][...] = token[...]
    for a, b in zip((wq, wk, wv, wo, dn), outs[:5]):
        b[...] = a[...].astype(f32)
    rows = outs[5].shape[0]
    width = up.shape[1]
    for t in range(outs[5].shape[1] // width):
        outs[5][:, t * width:(t + 1) * width] = up[t * rows:(t + 1) * rows, :].astype(f32)
    shard = lax.axis_index("seq") * 4 + lax.axis_index("shard")
    piece = outs[6].shape[1]
    r = lax.broadcasted_iota(jnp.int32, (width, PAIR), 0)
    c = lax.broadcasted_iota(jnp.int32, (width, PAIR), 1)
    pick = ((r == c + shard * piece) & (c < piece)).astype(f32)
    small = lax.dot_general(
        table[:8, :], pick, (((1,), (0,)), ((), ())), precision=lax.Precision.HIGHEST,
        preferred_element_type=f32,
    )
    for i in range(8):
        outs[6 + i][...] = small[i:i + 1, :piece]
    wide = outs[14].shape[1]
    per = width // wide
    at = pl.multiple_of((shard % per) * wide, wide)
    outs[14][...] = table[pl.ds(8 + shard // per, 1), pl.ds(at, wide)]


def finish(dn, up, wo, wq, wk, wv, table, token, wide):
    width = table.shape[1]
    f32 = jnp.float32
    S = jax.ShapeDtypeStruct
    piece = width // 8
    chunks = up.shape[0] // piece
    out = pl.pallas_call(
        finish_kernel,
        out_shape=(
            *[S(a.shape, f32) for a in (wq, wk, wv, wo, dn)], S((piece, chunks * width), f32),
            *[S((1, piece), f32)] * 8, S((1, wide), f32), S(token.shape, token.dtype),
        ),
        in_specs=[VM] * 8,
        out_specs=(VM,) * 16,
        compiler_params=pltpu.CompilerParams(vmem_limit_bytes=60 << 20),
        name="finish",
    )(dn, up, wo, wq, wk, wv, table, token)
    return out[15], list(out[:6]) + [a.reshape(-1) for a in out[6:15]]


EPSILON = 1e-06
PLANE = ("seq", "shard")


def normalize(hidden, gain, shift):
    center = hidden - jnp.mean(hidden, axis=-1, keepdims=True)
    spread = jnp.mean(center * center, axis=-1, keepdims=True)
    return center * lax.rsqrt(spread + EPSILON) * gain + shift


def smooth_gate(hidden):
    return jax.nn.gelu(hidden, approximate=False)


def mm(left, right):
    return jnp.dot(left, right, preferred_element_type=jnp.float32)


def contract_rows(left, right):
    return dot(left, right, 0, 0)


def times_transpose(left, right):
    return dot(left, right, 1, 1)


def tuned_plane():
    return lax.axis_size("seq") == 2 and lax.axis_size("shard") == 4 and lax.axis_size("blk") == 4


def total(g):
    part = lax.psum_scatter(g.astype(jnp.bfloat16), PLANE, scatter_dimension=0, tiled=True)
    return lax.psum(part, "blk").astype(jnp.float32)


def whole_line(
    inputs, seg, live, mats, vecs, cotangent, codes, own_codes, start,
):
    rows, width = inputs.shape
    length = seg.shape[0]
    scale = HEAD_DIM ** (-0.5)
    xs = lax.all_gather(inputs, "blk", axis=0, tiled=True)
    wq, wk, wv, wo, wup, wdn = [lax.all_gather(w, PLANE, axis=0, tiled=True) for w in mats]
    whole = [lax.all_gather(v, PLANE, axis=0, tiled=True).astype(jnp.float32) for v in vecs]
    bq, bv, bo, g1, s1, bdn, g2, s2, bup = whole
    own_seg = lax.dynamic_slice_in_dim(seg, start, rows)
    low = jnp.sum((seg < own_seg[0]).astype(jnp.int32))
    high = jnp.sum((seg <= own_seg[rows - 1]).astype(jnp.int32))
    span = jnp.stack([low // TILE, (high + TILE - 1) // TILE])
    q_all = ((mm(xs, wq) + bq) * scale).astype(jnp.bfloat16)
    k_all = mm(xs, wk).astype(jnp.bfloat16)
    v_all = (mm(xs, wv) + bv).astype(jnp.bfloat16)
    q, k, v = [lax.dynamic_slice_in_dim(a, start, rows) for a in (q_all, k_all, v_all)]
    summed, attended, lse = attention(q, k_all, v_all, codes, own_codes, span)

    first_sum = inputs.astype(jnp.float32) + (mm(attended, wo) + bo)
    first_norm, first_pull = jax.vjp(normalize, first_sum, g1, s1)
    first_low = first_norm.astype(jnp.bfloat16)
    hidden = mm(first_low, wup) + bup
    gated, gate_pull = jax.vjp(smooth_gate, hidden)
    gated_low = gated.astype(jnp.bfloat16)
    second_sum = first_norm + (mm(gated_low, wdn) + bdn)
    result, second_pull = jax.vjp(normalize, second_sum, g2, s2)
    second_grad, g2_grad, s2_grad = second_pull(cotangent.astype(jnp.float32))
    bdn_grad = jnp.sum(second_grad, axis=0)
    second_low = second_grad.astype(jnp.bfloat16)
    wdn_grad = contract_rows(gated_low, second_low)
    (hidden_grad,) = gate_pull(times_transpose(second_low, wdn))
    bup_grad = jnp.sum(hidden_grad, axis=0)
    hidden_low = hidden_grad.astype(jnp.bfloat16)
    wup_grad = contract_rows(first_low, hidden_low)
    norm_grad = second_grad + times_transpose(hidden_low, wup)
    first_grad, g1_grad, s1_grad = first_pull(norm_grad)
    bo_grad = jnp.sum(first_grad, axis=0)
    first_grad_low = first_grad.astype(jnp.bfloat16)
    wo_grad = contract_rows(attended, first_grad_low)
    do = times_transpose(first_grad_low, wo).astype(jnp.bfloat16)

    stats, delta = row_stats(do, summed, lse)
    do_all, stats_all = [lax.all_gather(a, "blk", axis=0) for a in (do, stats)]
    stats_all = jnp.transpose(stats_all, (1, 2, 0, 3)).reshape(stats.shape[0], 8, length)
    dq, dk, dv = attention_grad(
        q, k, v, do, lse, delta, q_all, k_all, v_all, do_all.reshape(length, width), stats_all,
        codes, own_codes, span,
    )
    r = dq * scale
    rq, rk, rv = [a.astype(jnp.bfloat16) for a in (r, dk, dv)]
    token_grad = first_grad + times_transpose(rq, wq) + times_transpose(rk, wk) + times_transpose(rv, wv)
    grads = [contract_rows(inputs, a) for a in (rq, rk, rv)] + [wo_grad, wdn_grad, wup_grad]
    vectors = [
        jnp.sum(r, axis=0), jnp.sum(dv, axis=0), bo_grad, g1_grad, s1_grad, bdn_grad, g2_grad, s2_grad, bup_grad,
    ]
    return result.astype(jnp.bfloat16), token_grad.astype(jnp.bfloat16), [total(g) for g in grads + vectors]


def tuned_line(inputs, mats, vecs, cotangent, codes, own_codes, nb):
    out = forward(inputs, codes, own_codes, mats, vecs, nb)
    wq, wk, wv, wo, wup, wdn, q_all, k_all, v_all, summed, attended, lse, table, bup = out
    out = middle(attended, inputs, cotangent, summed, lse, table, bup, wo, wup, wdn)
    result, rest, do, stats, delta, table, gdn, gup, gwo = out
    width = inputs.shape[1]
    early = [g.reshape(2, 2, 2, -1, width) for g in (gdn, gup, gwo)]
    token_grad, table, rdn, rup, ro, rwq, rwk, rwv = backward(
        codes, own_codes, do, stats, lse, delta, inputs, rest, table, q_all, k_all, v_all, [wq, wk, wv], early, nb,
    )
    token_grad, sums = finish(rdn, rup, ro, rwq, rwk, rwv, table, token_grad, vecs[8].shape[0])
    return result, token_grad, sums


def per_device(
    tokens, segments, live_mask, query_weight, key_weight, value_weight, out_weight,
    query_bias, value_bias, out_bias, first_gain, first_shift, up_weight, up_bias,
    down_weight, down_bias, second_gain, second_shift, cotangent,
):
    inputs = tokens[0]
    rows = inputs.shape[0]
    nb = lax.axis_size("blk")
    seg, live = segments[0], live_mask[0]
    start = lax.axis_index("blk") * rows
    codes = jnp.where(live > 0, seg, -1 - jnp.arange(seg.shape[0], dtype=jnp.int32))
    own_codes = lax.dynamic_slice_in_dim(codes, start, rows)
    mats = [query_weight, key_weight, value_weight, out_weight, up_weight, down_weight]
    vecs = [query_bias, value_bias, out_bias, first_gain, first_shift, down_bias, second_gain, second_shift, up_bias]
    if tuned_plane():
        result, token_grad, sums = tuned_line(inputs, mats, vecs, cotangent[0], codes, own_codes, nb)
    else:
        result, token_grad, sums = whole_line(
            inputs, seg, live, mats, vecs, cotangent[0], codes, own_codes, start
        )
    rwq, rwk, rwv, ro, rdn, rup, rbq, rbv, rbo, rg1, rs1, rbdn, rg2, rs2, rbup = sums
    return (
        result[None], token_grad[None],
        rwq, rwk, rwv, ro, rbq, rbv, rbo, rg1, rs1, rup, rbup, rdn, rbdn, rg2, rs2,
    )


def solution(mesh):
    flat = P(PLANE, "blk", None)
    mat = P(PLANE, None)
    vec = P(PLANE)
    return jax.shard_map(
        per_device,
        mesh=mesh,
        in_specs=(
            flat, mat, mat, mat, mat, mat, mat, vec, vec, vec, vec, vec, mat, vec, mat, vec, vec, vec, flat,
        ),
        out_specs=(flat, flat, mat, mat, mat, mat, vec, vec, vec, vec, vec, mat, vec, mat, vec, vec, vec),
        check_vma=False,
    )
```

profile of v0, /device:TPU:0, one launch (start us, length us, event | category | flops | bytes accessed | tf_op | source)
XLA Modules:
  0.0 260.6 jit_solution(11438412020067071329)
XLA Ops:
  0.7 1.2 reshape.152.refs_17_
  1.9 0.7 broadcast_compare_fusion
  2.6 1.3 subtract_select_fusion.refs_2_.refs_1_
  4.0 0.8 dynamic-slice_select_fusion
  4.7 0.9 copy.36.refs_1_.refs_0_
  5.6 79.6 %forward.1 = (bf16[768,768]{1,0:T(8,128)(2,1)}, bf16[768,768]{1,0:T(8,128)(2,1)}, bf16[768,768]{1,0:T(8,128)(2,1)}, bf16[768,768]{1,0:T(8,128)(2,1)}, bf16[768,3...) custom-call(bf16[512,768]{1,0:T(8,128)(2,1)} %bitcast.27, ...), custom_call_target="tpu_custom_call" | custom-call | tf_op jit(solution)/shard_map/forward/pallas_call | solution.py:792
  85.2 42.4 %middle.1 = (bf16[512,768]{1,0:T(8,128)(2,1)}, f32[512,768]{1,0:T(8,128)}, bf16[512,768]{1,0:T(8,128)(2,1)}, f32[6,8,512]{2,1,0:T(8,128)}, f32[512,768]{1,0:T(8,...) custom-call(bf16[512,768]{1,0:T(8,128)(2,1)} %get-tuple-element.64.a, ...), custom_call_target="tpu_custom_call" | custom-call | tf_op jit(solution)/shard_map/middle/pallas_call | solution.py:990
  127.6 127.7 %backward.1 = (bf16[512,768]{1,0:T(8,128)(2,1)}, f32[16,768]{1,0:T(8,128)}, bf16[384,768]{1,0:T(8,128)(2,1)}, bf16[384,768]{1,0:T(8,128)(2,1)}, bf16[96,768]{1,0...) custom-call(s32[512,1]{1,0:T(8,128)} %copy.36.refs_1_.refs_0_, ...), custom_call_target="tpu_custom_call" | custom-call | tf_op jit(solution)/shard_map/backward/pallas_call | solution.py:1259
  255.3 4.0 %finish.1 = (f32[96,768]{1,0:T(8,128)}, f32[96,768]{1,0:T(8,128)}, f32[96,768]{1,0:T(8,128)}, f32[96,768]{1,0:T(8,128)}, f32[384,768]{1,0:T(8,128)}, /*index=5*/...) custom-call(bf16[384,768]{1,0:T(8,128)(2,1)} %get-tuple-element.87.d, ...), custom_call_target="tpu_custom_call" | custom-call | tf_op jit(solution)/shard_map/finish/pallas_call | solution.py:1318
  259.4 1.3 reduce.1
where the time goes:
time: 261 us
  Pallas kernels  254 us (97%)
  other arithmetic  4.08 us (2%)
    pallas_call x1, Pallas kernels, backward(): pl.pallas_call(functools.partial(backward_kernel, nb), out_shape=(jax.Sha...  128 us
    pallas_call x1, Pallas kernels, forward(): pl.pallas_call(functools.partial(forward_kernel, nb), out_shape=(*mats, e...  79.6 us
    pallas_call x1, Pallas kernels, middle(): pl.pallas_call(middle_kernel, out_shape=(S((n, width), bf), S((n, width),...  42.4 us

commit v1 on v0

--- a/solution.py
+++ b/solution.py
@@ -34,7 +34,7 @@
         return (j, self.s, self.h)
 
 
-def enter(p, nb, plane, line):
+def greet(p, nb, plane, line):
     bar = pltpu.get_barrier_semaphore()
     count = 0
     if plane:
@@ -56,7 +56,11 @@
             def _():
                 pl.semaphore_signal(bar, inc=1, device_id=p.z(j), device_id_type=MESH)
         count = count + nb - 1
-    pl.semaphore_wait(bar, count)
+    return lambda: pl.semaphore_wait(bar, count)
+
+
+def enter(p, nb, plane, line):
+    greet(p, nb, plane, line)()
 
 
 def rcopy(src, dst, ss, rs, dev):
@@ -164,6 +168,14 @@
     lax.fori_loop(0, count, once, 0)
 
 
+def code_tables(seg, live, rows, col, place):
+    nb, _, n = rows.shape
+    ids = jnp.where(live[...] > 0, seg[...], -1 - lax.broadcasted_iota(jnp.int32, seg.shape, 1)).astype(jnp.float32)
+    for j in range(nb):
+        rows[j] = ids[:, j * n:(j + 1) * n]
+    col[...] = jnp.broadcast_to(rows[place], (128, n)).T[:, :1]
+
+
 def turn(b, nb, i):
     far = (i + 1) // 2
     j = jnp.where(i % 2 == 1, b - far, b + far)
@@ -180,27 +192,103 @@
         lax.fori_loop(0, rows // chunk, step, 0)
 
 
-class PlaneReduce:
-    def __init__(self, p, nb, g, out, buf, stage, ss, rs, ls):
-        self.p, self.nb = p, nb
-        self.P, self.BX, self.BY, self.CX, self.CY, self.Z = buf
-        self.O = out
+def add_low(a, b):
+    return (a.astype(jnp.float32) + b.astype(jnp.float32)).astype(a.dtype)
+
+
+def add_into(dst, src):
+    def body(r):
+        rows = pl.ds(r, 48)
+        dst[rows] = add_low(dst[rows], src[rows])
+    row_loop(dst.shape[0], 48, body)
+
+
+class PlaneSum:
+    def __init__(self, p, g, buf, stage, ss, rs, ls):
+        self.p = p
+        self.P, self.BX, self.BY, self.CX, self.CY = buf
         self.R, self.C = g.shape[-2:]
-        self.dt = g.dtype
-        self.ss, self.rs = ss, rs
         h = self.R // 2
         self.h = h
         lo, hi = pl.ds(0, h), pl.ds(h, h)
-        self.chunk = 16 if self.C > 1024 else 48
         self.g = g
         self.stage = stage
+        self.ss, self.rs = ss, rs
         self.own = None if stage is None else pltpu.make_async_copy(g.at[:, :, p.c], stage, ls)
-        self.cA = rcopy(g.at[:, :, 1 - p.c], self.P, ss.at[0], rs.at[0], p.C)
         self.cBX = rcopy(self.P.at[:, 1 - p.x, lo], self.BX, ss.at[1], rs.at[1], p.X)
         self.cBY = rcopy(self.P.at[1 - p.s, :, hi], self.BY, ss.at[2], rs.at[2], p.Y)
         self.cCX = rcopy(self.P.at[p.s, 1 - p.x, hi], self.CX, ss.at[3], rs.at[3], p.X)
         self.cCY = rcopy(self.P.at[1 - p.s, p.x, lo], self.CY, ss.at[4], rs.at[4], p.Y)
-        self.F = self.P.at[p.s, p.x]
+        self.total = self.P.at[p.s, p.x]
+
+    def piece(self, t):
+        s, x = t // 2, t % 2
+        return rcopy(self.g.at[s, x, 1 - self.p.c], self.P.at[s, x], self.ss.at[5 + t], self.rs.at[5 + t], self.p.C)
+
+    def _core(self):
+        return rcopy(self.g.at[:, :, 1 - self.p.c], self.P, self.ss.at[0], self.rs.at[0], self.p.C)
+
+    def a_start(self):
+        self._core().start()
+
+    def own_start(self):
+        self.own.start()
+
+    def b_start(self, pieces=False):
+        if self.own is not None:
+            self.own.wait()
+        if not pieces:
+            self._core().wait_recv()
+
+        def block(i, _):
+            s, x = i // 2, i % 2
+            if pieces:
+                self.piece(i).wait_recv()
+
+            def body(r):
+                rows = pl.ds(r, 48)
+                mine = self.g[s, x, self.p.c, rows] if self.stage is None else self.stage[s, x, rows]
+                self.P[s, x, rows] = add_low(mine, self.P[s, x, rows])
+            row_loop(self.R, 48, body)
+            return 0
+        lax.fori_loop(0, 4, block, 0)
+        self.cBX.start()
+        self.cBY.start()
+
+    def c_start(self):
+        p, h = self.p, self.h
+        lo, hi = pl.ds(0, h), pl.ds(h, h)
+        self.cBX.wait_recv()
+        add_into(self.P.at[1 - p.s, p.x, lo], self.BX.at[1 - p.s])
+        self.cCY.start()
+        self.cBY.wait_recv()
+        add_into(self.P.at[p.s, 1 - p.x, hi], self.BY.at[1 - p.x])
+        self.cCX.start()
+        add_into(self.P.at[p.s, p.x, lo], self.BX.at[p.s])
+        add_into(self.P.at[p.s, p.x, hi], self.BY.at[p.x])
+
+    def end(self):
+        h = self.h
+        self.cCY.wait_recv()
+        add_into(self.total.at[pl.ds(0, h)], self.CY)
+        self.cCX.wait_recv()
+        add_into(self.total.at[pl.ds(h, h)], self.CX)
+
+    def drain(self, pieces=False):
+        for k in (self.cBX, self.cBY, self.cCX, self.cCY):
+            k.wait_send()
+        if pieces:
+            for t in range(4):
+                self.piece(t).wait_send()
+        else:
+            self._core().wait_send()
+
+
+class LineSum:
+    def __init__(self, p, nb, part, out, Z, ss, rs):
+        self.p, self.nb, self.F, self.O, self.Z, self.ss, self.rs = p, nb, part, out, Z, ss, rs
+        self.R, self.C = part.shape
+        self.h = self.R // 2
 
     def quarter(self, ref, j):
         R, C = self.R, self.C
@@ -209,92 +297,16 @@
             r, c = pl.multiple_of(r, R // 2), pl.multiple_of(c, C // 2)
         return ref.at[pl.ds(r, R // 2), pl.ds(c, C // 2)]
 
-    def a_start(self):
-        self.cA.start()
-
-    def own_start(self):
-        self.own.start()
-
-    def b_start(self):
-        if self.own is not None:
-            self.own.wait()
-        self.cA.wait_recv()
-
-        def block(i, _):
-            s, x = i // 2, i % 2
-
-            def body(r):
-                rows = pl.ds(r, self.chunk)
-                mine = self.g[s, x, self.p.c, rows] if self.stage is None else self.stage[s, x, rows]
-                self.P[s, x, rows] = (
-                    mine.astype(jnp.float32) + self.P[s, x, rows].astype(jnp.float32)
-                ).astype(self.dt)
-            row_loop(self.R, self.chunk, body)
-            return 0
-        lax.fori_loop(0, 4, block, 0)
-        self.cBX.start()
-        self.cBY.start()
-
-    def _add(self, dst, src):
-        chunk = min(self.chunk * 2, self.h)
-
-        def body(r):
-            rows = pl.ds(r, chunk)
-            dst[rows] = (dst[rows].astype(jnp.float32) + src[rows].astype(jnp.float32)).astype(self.dt)
-        row_loop(self.h, chunk if self.h % chunk == 0 else self.h, body)
-
-    def c_start(self):
-        p, h = self.p, self.h
-        lo, hi = pl.ds(0, h), pl.ds(h, h)
-        self.cBX.wait_recv()
-        self._add(self.P.at[1 - p.s, p.x, lo], self.BX.at[1 - p.s])
-        self.cCY.start()
-        self.cBY.wait_recv()
-        self._add(self.P.at[p.s, 1 - p.x, hi], self.BY.at[1 - p.x])
-        self.cCX.start()
-        self._add(self.P.at[p.s, p.x, lo], self.BX.at[p.s])
-        self._add(self.P.at[p.s, p.x, hi], self.BY.at[p.x])
-
-
-    def _right(self, j):
-        return rcopy(self.quarter(self.F, j), self.Z.at[j], self.ss.at[5 + j], self.rs.at[5 + j], self.p.R)
-
-    def _left(self, j, last):
-        slot = self.nb if last else j
-        k = 5 + self.nb + j
-        return rcopy(self.quarter(self.F, j), self.Z.at[slot], self.ss.at[k], self.rs.at[k], self.p.L)
-
-    def plane_end(self):
-        h = self.h
-        self.cCY.wait_recv()
-        self._add(self.F.at[pl.ds(0, h)], self.CY)
-        self.cCX.wait_recv()
-        self._add(self.F.at[pl.ds(h, h)], self.CX)
-
-    def hop(self, t):
-        nb, p = self.nb, self.p
-        if t == 0:
-            self.plane_end()
-
-        @pl.when(p.b == t)
-        def _():
-            for j in range(nb - 1, t, -1):
-                if t > 0:
-                    self._right(j).wait_recv()
-                    self._add(self.quarter(self.F, j), self.Z.at[j])
-                self._right(j).start()
-
-        @pl.when(p.b == nb - 1 - t)
-        def _():
-            for j in range(nb - 1 - t):
-                if t > 0:
-                    self._left(j, False).wait_recv()
-                    self._add(self.quarter(self.F, j), self.Z.at[j])
-                self._left(j, j == nb - 2 - t).start()
+    def _send(self, j, slot):
+        return rcopy(self.quarter(self.F, j), self.Z.at[slot], self.ss.at[j], self.rs.at[slot], self.p.z(j))
+
+    def start(self):
+        for j in range(self.nb):
+            pl.when(self.p.b != j)(self._send(j, self.p.b).start)
 
     def _spread(self, t):
         p, nb = self.p, self.nb
-        k = 5 + 2 * nb + 2 * t
+        k = nb + 2 * t
         r, l = p.b - t, p.b + t
         qr = self.quarter(self.O, jnp.maximum(r, 0))
         ql = self.quarter(self.O, jnp.minimum(l, nb - 1))
@@ -302,44 +314,136 @@
         left = rcopy(ql, ql, self.ss.at[k + 1], self.rs.at[k + 1], p.L)
         return right, left, (r >= 0) & (p.b < nb - 1), (l <= nb - 1) & (p.b > 0)
 
-    def _spread_recv(self, t):
+    def _spread_recv(self, t, forwarded):
         right, left, _, _ = self._spread(t)
         p, nb = self.p, self.nb
-        pl.when(p.b - 1 - t >= 0)(right.wait_recv)
-        pl.when(p.b + 1 + t <= nb - 1)(left.wait_recv)
+        hands_right, hands_left = p.b < nb - 1, p.b > 0
+        if t == nb - 2:
+            hands_right, hands_left = False, False
+        if forwarded:
+            pl.when((p.b - 1 - t >= 0) & hands_right)(right.wait_recv)
+            pl.when((p.b + 1 + t <= nb - 1) & hands_left)(left.wait_recv)
+        else:
+            pl.when((p.b - 1 - t >= 0) & jnp.logical_not(hands_right))(right.wait_recv)
+            pl.when((p.b + 1 + t <= nb - 1) & jnp.logical_not(hands_left))(left.wait_recv)
+
+    def _sum(self):
+        p, nb = self.p, self.nb
+        mine = self.quarter(self.F, p.b)
+        total = self.quarter(self.O, p.b)
+        for j in range(nb):
+            pl.when(p.b != j)(self._send(j, j).wait_recv)
+
+        def body(r):
+            rows = pl.ds(r, 48)
+            acc = mine[rows].astype(jnp.float32)
+            for d in range(1, nb):
+                acc = acc + self.Z[(p.b + d) % nb, rows].astype(jnp.float32)
+            total[rows] = acc.astype(mine.dtype)
+        row_loop(self.h, 48, body)
 
     def spread(self, t):
-        p, nb = self.p, self.nb
         if t == 0:
-            mine = self.quarter(self.F, p.b)
-            for j in range(nb):
-                @pl.when(p.b == j)
-                def _():
-                    if j > 0:
-                        self._right(j).wait_recv()
-                        self._add(mine, self.Z.at[j])
-                    if j < nb - 1:
-                        self._left(j, True).wait_recv()
-                        self._add(mine, self.Z.at[nb])
-            total = self.quarter(self.O, p.b)
-
-            def body(r):
-                rows = pl.ds(r, self.chunk)
-                total[rows] = mine[rows]
-            row_loop(self.h, self.chunk, body)
+            self._sum()
         else:
-            self._spread_recv(t - 1)
+            self._spread_recv(t - 1, True)
         right, left, cr, cl = self._spread(t)
         pl.when(cr)(right.start)
         pl.when(cl)(left.start)
 
     def finish(self):
-        self._spread_recv(self.nb - 2)
+        for t in range(self.nb - 1):
+            self._spread_recv(t, False)
+
+    def drain(self):
+        for j in range(self.nb):
+            pl.when(self.p.b != j)(self._send(j, self.p.b).wait_send)
+        for t in range(self.nb - 1):
+            right, left, cr, cl = self._spread(t)
+            pl.when(cr)(right.wait_send)
+            pl.when(cl)(left.wait_send)
+
+
+class DirectSum(LineSum):
+    def _share(self, j, slot):
+        q = self.quarter(self.O, slot)
+        return rcopy(q, q, self.ss.at[self.nb + j], self.rs.at[self.nb + slot], self.p.z(j))
+
+    def share(self):
+        self._sum()
+        for j in range(self.nb):
+            pl.when(self.p.b != j)(self._share(j, self.p.b).start)
+
+    def finish(self):
+        for j in range(self.nb):
+            pl.when(self.p.b != j)(self._share(j, j).wait_recv)
+
+    def drain(self):
+        for j in range(self.nb):
+            @pl.when(self.p.b != j)
+            def _():
+                self._send(j, self.p.b).wait_send()
+                self._share(j, self.p.b).wait_send()
+
+
+class ChainSum(LineSum):
+    def _right(self, j):
+        return rcopy(self.quarter(self.F, j), self.Z.at[j], self.ss.at[j], self.rs.at[j], self.p.R)
+
+    def _left(self, j, last):
+        slot = self.nb if last else j
+        k = 3 * self.nb - 2 + j
+        return rcopy(self.quarter(self.F, j), self.Z.at[slot], self.ss.at[k], self.rs.at[k], self.p.L)
+
+    def start(self):
+        self.hop(0)
+
+    def hop(self, t):
+        nb, p = self.nb, self.p
+
+        @pl.when(p.b == t)
+        def _():
+            for j in range(nb - 1, t, -1):
+                if t > 0:
+                    self._right(j).wait_recv()
+                    add_into(self.quarter(self.F, j), self.Z.at[j])
+                self._right(j).start()
+
+        @pl.when(p.b == nb - 1 - t)
+        def _():
+            for j in range(nb - 1 - t):
+                if t > 0:
+                    self._left(j, False).wait_recv()
+                    add_into(self.quarter(self.F, j), self.Z.at[j])
+                self._left(j, j == nb - 2 - t).start()
+
+    def _sum(self):
+        p, nb = self.p, self.nb
+        mine = self.quarter(self.F, p.b)
+        total = self.quarter(self.O, p.b)
+        for j in range(nb):
+            @pl.when(p.b == j)
+            def _():
+                if j > 0:
+                    self._right(j).wait_recv()
+                if j < nb - 1:
+                    self._left(j, True).wait_recv()
+
+        @pl.when(p.b > 0)
+        def _():
+            add_into(mine, self.Z.at[p.b])
+
+        @pl.when(p.b < nb - 1)
+        def _():
+            add_into(mine, self.Z.at[nb])
+
+        def body(r):
+            rows = pl.ds(r, 48)
+            total[rows] = mine[rows]
+        row_loop(self.h, 48, body)
 
     def drain(self):
         nb, p = self.nb, self.p
-        for k in (self.cA, self.cBX, self.cBY, self.cCX, self.cCY):
-            k.wait_send()
         for t in range(nb - 1):
             @pl.when(p.b == t)
             def _():
@@ -355,24 +459,23 @@
             pl.when(cl)(left.wait_send)
 
 
-def reduce_scratch(shape, dt, nb):
+def plane_scratch(shape):
     R, C = shape
     h = R // 2
-    return [
-        pltpu.VMEM((2, 2, R, C), dt),
-        pltpu.VMEM((2, h, C), dt),
-        pltpu.VMEM((2, h, C), dt),
-        pltpu.VMEM((h, C), dt),
-        pltpu.VMEM((h, C), dt),
-        pltpu.VMEM((nb + 1, h, C // 2), dt),
-    ]
-
-
-NBUF = 6
-
-
-def reduce_sems(nb):
-    return 5 + 2 * nb + 2 * (nb - 1)
+    sizes = ((2, 2, R, C), (2, h, C), (2, h, C), (h, C), (h, C))
+    return [pltpu.VMEM(s, jnp.bfloat16) for s in sizes]
+
+
+def line_scratch(shape, nb):
+    return pltpu.VMEM((nb + 1, shape[0] // 2, shape[1] // 2), jnp.bfloat16)
+
+
+PLANE_BUFS = 5
+PLANE_SEMS = 9
+
+
+def line_sems(nb):
+    return 2 * nb + 2 * (nb - 1)
 
 
 class TableSum:
@@ -623,15 +726,15 @@
 
 
 def forward_kernel(nb, *refs):
-    x_ref, codes, rows = refs[:3]
+    x_ref, seg, live = refs[:3]
     shards_in = refs[3:9]
     vecs_in = refs[9:18]
     wq_o, wk_o, wv_o, wo_o, wup_o, wdn_o = refs[18:24]
     q_o, k_o, v_o = refs[24:27]
     o_ref, ob_ref, lse_ref, vec_ref, bup_ref = refs[27:32]
     rest = refs[32:]
-    x_all, wq, wk, wv, pack, packs, q, k, v, m_ref, l_ref = rest[:11]
-    zs, zr, gs, gr, gl, ws, es = rest[11:]
+    x_all, wq, wk, wv, pack, packs, q, k, v, m_ref, l_ref, codes, rows = rest[:13]
+    zs, zr, gs, gr, gl, ws, es = rest[13:]
     n, width = x_ref.shape
     pairs = width // PAIR
     p = Place()
@@ -650,6 +753,7 @@
     line.start(0)
     for c in g[:5]:
         c.start()
+    code_tables(seg, live, rows, codes, p.b)
     for c in g[:4]:
         c.forward()
     g[5].start()
@@ -781,7 +885,7 @@
         c.drain()
 
 
-def forward(x, codes, own_codes, weights, vecs, nb):
+def forward(x, seg, live, weights, vecs, nb):
     n, width = x.shape
     hidden = weights[4].shape[1]
     bf, f32 = jnp.bfloat16, jnp.float32
@@ -803,6 +907,7 @@
             pltpu.VMEM((2 * VEC_ROWS, PAIR), f32), pltpu.VMEM((16 * VEC_ROWS, PAIR), f32),
             pltpu.VMEM((nb, n, width), bf), pltpu.VMEM((nb, n, width), bf), pltpu.VMEM((nb, n, width), bf),
             pltpu.VMEM((width // HEAD_DIM, n, PAIR), f32), pltpu.VMEM((width // HEAD_DIM, n, PAIR), f32),
+            pltpu.VMEM((n, 1), f32), pltpu.VMEM((nb, 1, n), f32),
             dma((2, nb - 1)), dma((2, nb - 1)), dma((7, 9)), dma((7, 9)), dma((7,)), dma((4,)), dma((3, 2 * nb)),
         ],
         compiler_params=pltpu.CompilerParams(
@@ -810,7 +915,7 @@
         ),
         name="forward",
     )(
-        x, own_codes.reshape(n, 1), codes.reshape(nb, 1, n), *weights, *[v.reshape(1, -1) for v in vecs]
+        x, seg, live, *weights, *[v.reshape(1, -1) for v in vecs]
     )
 
 
@@ -870,7 +975,7 @@
     def column_sum(a):
         return jnp.sum(a, axis=0, keepdims=True)
 
-    blocks = 4
+    blocks = 2
     m = n // blocks
 
     def rows_of(i):
@@ -955,7 +1060,9 @@
         rest_ref[r, :] = dh
         low = dh.astype(bf)
         low_ref[r, :] = low
-        do_ref[r, :] = dot(low, wo[...], 1, 1).astype(bf)
+        do = dot(low, wo[...], 1, 1).astype(bf)
+        do_ref[r, :] = do
+        table_ref[1:2, :] += column_sum(do.astype(f32))
         return 0
     lax.fori_loop(0, blocks, third, 0)
 
@@ -1008,6 +1115,9 @@
     )(att, x, cot, o, lse, vecs, bup, wo, wup, wdn)
 
 
+PAIR_GROUP = 2
+
+
 class AttentionGrad:
     def __init__(self, codes, rows, q, k, v, g, lse, delta, stats, own, dq, dk, dv):
         self.codes, self.rows = codes, rows
@@ -1018,10 +1128,10 @@
         self.n = dq.shape[0]
         self.pairs = dq.shape[1] // PAIR
 
-    def queries(self, j):
+    def queries(self, j, group):
         own = self.own
 
-        def pair(h, _):
+        def pair(h):
             left = left_lanes((self.n, PAIR))
             lanes = pl.ds(pl.multiple_of(h * PAIR, PAIR), PAIR)
             mask = self.codes[...] == self.rows[j]
@@ -1037,14 +1147,14 @@
                 ds = (p * (dp - delta[:, at])).astype(jnp.bfloat16)
                 parts.append(dot(ds, k, 1, 0))
             self.dq[:, lanes] += jnp.where(left, parts[0], parts[1])
-            return 0
-
-        lax.fori_loop(0, self.pairs, pair, 0, unroll=2)
-
-    def keys(self, j):
+
+        for i in range(PAIR_GROUP):
+            pair(group * PAIR_GROUP + i)
+
+    def keys(self, j, group):
         own = self.own
 
-        def pair(h, _):
+        def pair(h):
             left = left_lanes((self.n, PAIR))
             lanes = pl.ds(pl.multiple_of(h * PAIR, PAIR), PAIR)
             mask = self.codes[...] == self.rows[j]
@@ -1060,31 +1170,33 @@
                 dks.append(dot(dst, q, 1, 0))
             self.dk[:, lanes] += jnp.where(left, dks[0], dks[1])
             self.dv[:, lanes] += jnp.where(left, dvs[0], dvs[1])
-            return 0
-
-        lax.fori_loop(0, self.pairs, pair, 0, unroll=2)
+
+        for i in range(PAIR_GROUP):
+            pair(group * PAIR_GROUP + i)
 
 
 TABLE = 16
 
 
 def backward_kernel(nb, *refs):
-    codes, rows, g_own, st_own, lse, delta, x_ref, rest_ref, table = refs[:9]
+    seg, live, g_own, st_own, lse, delta, x_hbm, rest_hbm, table = refs[:9]
     q_hbm, k_hbm, v_hbm, wq_hbm, wk_hbm, wv_hbm = refs[9:15]
     early = refs[15:18]
     token_ref, table_out = refs[18:20]
-    outs = refs[20:26]
-    rest = refs[26:]
-    q, k, v, g, stats, dq, dk, dv, wq, wk, wv, gw, stage_a, stage_b, tab, tsum, tline = rest[:17]
-    bufs = rest[17:17 + 6 * NBUF]
-    zs, zr, ls, ss, rs, rls, ts, tr = rest[17 + 6 * NBUF:]
+    outs = refs[20:24]
+    rest = refs[24:]
+    q, k, v, g, stats, dq, dk, dv, wq, wk, wv, gw, stage_dn, stage_up, tab, tsum, tline, x_ref, rest_ref, codes, rows = rest[:21]
+    zbufs = rest[21:25]
+    bufs = rest[25:25 + 4 * PLANE_BUFS]
+    zs, zr, ls, ps, pr, ds, dr, rls, ts, tr = rest[25 + 4 * PLANE_BUFS:]
     n, width = g_own.shape
     p = Place()
     loads = [
         pltpu.make_async_copy(a, b, ls.at[i])
         for i, (a, b) in enumerate((
             (k_hbm, k), (v_hbm, v), (q_hbm, q), (g_own, g.at[p.b]), (st_own, stats.at[p.b]),
-            (wq_hbm, wq), (wk_hbm, wk), (wv_hbm, wv),
+            (wq_hbm, wq), (wk_hbm, wk), (wv_hbm, wv), (x_hbm, x_ref), (rest_hbm, rest_ref),
+            (early[2], gw.at[0, :, :, :, pl.ds(gw.shape[4] // 2, gw.shape[4] // 2)]),
         ))
     ]
     for c in loads:
@@ -1094,28 +1206,33 @@
         LineGather(p, nb, g_own, g, zs.at[0], zr.at[0]),
         LineGather(p, nb, st_own, stats, zs.at[1], zr.at[1]),
     ]
-    sources = tuple(early) + tuple(gw.at[i] for i in range(3))
-    stages = (stage_a, stage_a, stage_b, None, None, None)
-    dn, up, wo, gq, gk, gv = [
-        PlaneReduce(
-            p, nb, sources[i], outs[i], bufs[NBUF * i:NBUF * (i + 1)],
-            None if stages[i] is None else stages[i].reshape(sources[i].shape[:2] + sources[i].shape[3:]),
-            ss.at[i], rs.at[i], rls.at[i],
+    sources = (early[0], early[1], gw.at[0], gw.at[1])
+    stages = (stage_dn, stage_up, None, None)
+    planes = [
+        PlaneSum(
+            p, sources[i], bufs[PLANE_BUFS * i:PLANE_BUFS * (i + 1)], stages[i], ps.at[i], pr.at[i], rls.at[min(i, 1)]
         )
-        for i in range(6)
+        for i in range(4)
     ]
+    dn, up, qo, kv = planes
+    chains = [
+        (DirectSum if i == 3 else ChainSum)(p, nb, planes[i].total, outs[i], zbufs[i], ds.at[i], dr.at[i])
+        for i in range(4)
+    ]
+    ldn, lup, lqo, lkv = chains
     vec = TableSum(p, nb, tab, tsum, tline, ts, tr)
     for c in lines:
         c.start(0)
-    for c in (dn, up, wo):
+    for c in (dn, up):
         c.a_start()
-    dn.own_start()
-    wo.own_start()
+        c.own_start()
     work = AttentionGrad(codes, rows, q, k, v, g, lse, delta, stats, p.b, dq, dk, dv)
+    code_tables(seg, live, rows, codes, p.b)
     for c in (dq, dk, dv):
         c[...] = jnp.zeros_like(c)
-    for i in (0, 1, 2, 3):
-        loads[i].wait()
+    for c in loads[:4]:
+        c.wait()
+    dn.b_start()
 
     low = k
     def slot(i):
@@ -1127,15 +1244,15 @@
             tab[row:row + 1, :] = jnp.sum(value, axis=0, keepdims=True)
         low[slot(i)] = value.astype(jnp.bfloat16)
 
-    def weight_grad(i):
+    def weight_grad(i, item, base):
         half = width // 2
+        r = width // 8
         for m in range(2):
             part = dot(x_ref[:, m * half:(m + 1) * half], low[slot(i)], 0, 0).astype(jnp.bfloat16)
-            r = gw.shape[-2]
             for a in range(2):
                 for b in range(2):
                     at = (2 * a + b) * r
-                    gw[i, m, a, b] = part[at:at + r]
+                    gw[item, m, a, b, base:base + r] = part[at:at + r]
 
     def hop(t, last=False):
         for c in lines:
@@ -1143,53 +1260,55 @@
             if not last:
                 c.start(t + 1)
 
+    groups = work.pairs // PAIR_GROUP
     staged(
-        nb,
+        nb * groups,
         {
-            1: [dn.b_start, up.own_start],
-            2: [up.b_start, wo.b_start, lambda: hop(0)],
-            3: [dn.c_start],
+            2: [up.b_start],
+            5: [lambda: hop(0)],
+            6: [dn.c_start],
         },
-        lambda i: work.queries((p.b + i) % nb),
+        lambda i: work.queries((p.b + i // groups) % nb, i % groups),
     )
-    for i in (4, 5, 6, 7):
-        loads[i].wait()
+    for c in loads[4:]:
+        c.wait()
     tab[...] = table[...]
     settle(0, dq, HEAD_DIM ** (-0.5), 0)
-    weight_grad(0)
-    gq.a_start()
+    vec.start()
+    weight_grad(0, 0, 0)
+    qo.a_start()
     hop(1)
     up.c_start()
 
     def keys(i):
-        ok, j = turn(p.b, nb, i)
-        pl.when(ok)(lambda: work.keys(j))
+        ok, j = turn(p.b, nb, i // groups)
+        pl.when(ok)(lambda: work.keys(j, i % groups))
+
+    def across(a, c):
+        a.end()
+        c.start()
 
     staged(
-        2 * nb - 1,
+        (2 * nb - 1) * groups,
         {
-            1: [gq.b_start, wo.c_start],
-            2: [lambda: dn.hop(0)],
-            3: [lambda: up.hop(0), lambda: wo.hop(0), gq.c_start, lambda: dn.hop(1)],
-            5: [lambda: up.hop(1), lambda: wo.hop(1), lambda: dn.hop(2), lambda: hop(2, True)],
+            2: [lambda: across(dn, ldn), qo.b_start],
+            5: [lambda: across(up, lup)],
+            6: [lambda: ldn.hop(1)],
+            8: [qo.c_start],
+            9: [lambda: lup.hop(1), lambda: ldn.hop(2)],
+            12: [lambda: across(qo, lqo), lambda: lup.hop(2), lambda: ldn.spread(0)],
+            15: [lambda: hop(2, True), lambda: lqo.hop(1), lambda: lup.spread(0), lambda: ldn.spread(1)],
+            18: [lambda: lqo.hop(2), lambda: lup.spread(1), lambda: ldn.spread(2)],
         },
         keys,
     )
     settle(1, dk, None, None)
-    settle(2, dv, None, 1)
-    vec.start()
-    weight_grad(1)
-    gk.a_start()
-    weight_grad(2)
-    gv.a_start()
-    up.hop(2)
-    wo.hop(2)
-    dn.spread(0)
+    weight_grad(1, 1, 0)
+    settle(2, dv, None, None)
+    weight_grad(2, 1, width // 8)
+    kv.a_start()
     vec.step(0)
-    gk.b_start()
-    gv.b_start()
-    gq.hop(0)
-    vec.step(1)
+    kv.b_start()
 
     part = 256
 
@@ -1202,92 +1321,77 @@
         return 0
     lax.fori_loop(0, width // part, columns, 0)
 
-    up.spread(0)
-    wo.spread(0)
-    dn.spread(1)
+    lqo.spread(0)
+    lup.spread(2)
+    vec.step(1)
+    kv.c_start()
+    lqo.spread(1)
     vec.step(2)
-    gk.c_start()
-    gv.c_start()
-    gq.hop(1)
-    up.spread(1)
-    wo.spread(1)
-    dn.spread(2)
-    gq.hop(2)
-    gk.hop(0)
-    gv.hop(0)
-    gq.spread(0)
-    gk.hop(1)
-    gv.hop(1)
-    up.spread(2)
-    wo.spread(2)
-    gk.hop(2)
-    gv.hop(2)
-    gq.spread(1)
-    gk.spread(0)
-    gv.spread(0)
-    gq.spread(2)
-    gk.spread(1)
-    gv.spread(1)
-    gk.spread(2)
-    gv.spread(2)
+    across(kv, lkv)
+    lqo.spread(2)
+    lkv.share()
     vec.finish(table_out)
-    every = (dn, up, wo, gq, gk, gv)
-    for c in every:
+    for c in chains:
         c.finish()
     for t in range(nb - 1):
         for c in lines:
             c.wait_send(t)
-    for c in every:
+    for c in planes:
+        c.drain()
+    for c in chains:
         c.drain()
     vec.drain()
 
 
-def backward(codes, own_codes, do, stats, lse, delta, x, rest, table, q_all, k_all, v_all, weights, early, nb):
+def backward(seg, live, do, stats, lse, delta, x, rest, table, q_all, k_all, v_all, weights, early, nb):
     n, width = do.shape
     bf, f32 = jnp.bfloat16, jnp.float32
-    late = jax.ShapeDtypeStruct((2, 2, 2, width // 8, width), bf)
-    kinds = list(early) + [late] * 3
+    pair = (2, 2, 2, width // 4, width)
+    sources = [early[0].shape, early[1].shape, pair, pair]
+    sums = [s[-2:] for s in sources]
     scratch = []
-    for g in kinds:
-        scratch += reduce_scratch(g.shape[-2:], bf, nb)
-    ns = reduce_sems(nb)
+    for s in sources:
+        scratch += plane_scratch(s[-2:])
+    ns = line_sems(nb)
     every = pltpu.VMEM((nb, n, width), bf)
     total = pltpu.VMEM((n, width), f32)
     square = pltpu.VMEM((width, width), bf)
     dma = pltpu.SemaphoreType.DMA
-    big, small = early[0].shape, early[2].shape
     return pl.pallas_call(
         functools.partial(backward_kernel, nb),
         out_shape=(
             jax.ShapeDtypeStruct((n, width), bf), jax.ShapeDtypeStruct((TABLE, width), f32),
-            *[jax.ShapeDtypeStruct(g.shape[-2:], bf) for g in kinds],
+            *[jax.ShapeDtypeStruct(s, bf) for s in sums],
         ),
-        in_specs=[VM] * 9 + [ANY] * 9,
-        out_specs=(VM,) * 8,
+        in_specs=[VM] * 6 + [ANY] * 2 + [VM] + [ANY] * 9,
+        out_specs=(VM,) * 6,
         scratch_shapes=[
             every, every, every, every, pltpu.VMEM((nb,) + stats.shape, f32), total, total, total,
-            square, square, square, pltpu.VMEM((3,) + late.shape, bf),
-            pltpu.VMEM(big[:2] + big[3:], bf), pltpu.VMEM(small[:2] + small[3:], bf),
+            square, square, square, pltpu.VMEM((2,) + pair, bf),
+            *[pltpu.VMEM(s[:2] + s[3:], bf) for s in sources[:2]],
             pltpu.VMEM((TABLE, width), f32), pltpu.VMEM((6, TABLE, width), f32), pltpu.VMEM((nb, TABLE, width), f32),
-        ] + scratch + [
-            dma((2, 2, nb - 1)), dma((2, 2, nb - 1)), dma((8,)), dma((6, ns)), dma((6, ns)), dma((3,)),
-            dma((3 + nb,)), dma((3 + nb,)),
+            pltpu.VMEM((n, width), bf), total, pltpu.VMEM((n, 1), f32), pltpu.VMEM((nb, 1, n), f32),
+            *[line_scratch(s, nb) for s in sums], *scratch,
+            dma((2, 2, nb - 1)), dma((2, 2, nb - 1)), dma((12,)), dma((4, PLANE_SEMS)), dma((4, PLANE_SEMS)),
+            dma((4, ns)), dma((4, ns)), dma((2,)), dma((3 + nb,)), dma((3 + nb,)),
         ],
         compiler_params=pltpu.CompilerParams(
             collective_id=4, has_side_effects=True, vmem_limit_bytes=63 << 20
         ),
         name="backward",
     )(
-        own_codes.reshape(n, 1), codes.reshape(nb, 1, n), do, stats, lse, delta, x, rest, table,
+        seg, live, do, stats, lse, delta, x, rest, table,
         q_all, k_all, v_all, *weights, *early,
     )
 
 
-def finish_kernel(dn, up, wo, wq, wk, wv, table, token, *outs):
+def finish_kernel(dn, up, qo, kv, table, token, *outs):
     f32 = jnp.float32
     outs[15][...] = token[...]
-    for a, b in zip((wq, wk, wv, wo, dn), outs[:5]):
-        b[...] = a[...].astype(f32)
+    n = outs[0].shape[0]
+    for i, (a, at) in enumerate(((qo, 0), (kv, 0), (kv, n), (qo, n))):
+        outs[i][...] = a[at:at + n, :].astype(f32)
+    outs[4][...] = dn[...].astype(f32)
     rows = outs[5].shape[0]
     width = up.shape[1]
     for t in range(outs[5].shape[1] // width):
@@ -1309,7 +1413,7 @@
     outs[14][...] = table[pl.ds(8 + shard // per, 1), pl.ds(at, wide)]
 
 
-def finish(dn, up, wo, wq, wk, wv, table, token, wide):
+def finish(dn, up, qo, kv, table, token, wide):
     width = table.shape[1]
     f32 = jnp.float32
     S = jax.ShapeDtypeStruct
@@ -1318,14 +1422,14 @@
     out = pl.pallas_call(
         finish_kernel,
         out_shape=(
-            *[S(a.shape, f32) for a in (wq, wk, wv, wo, dn)], S((piece, chunks * width), f32),
+            *[S((piece, width), f32)] * 4, S(dn.shape, f32), S((piece, chunks * width), f32),
             *[S((1, piece), f32)] * 8, S((1, wide), f32), S(token.shape, token.dtype),
         ),
-        in_specs=[VM] * 8,
+        in_specs=[VM] * 6,
         out_specs=(VM,) * 16,
         compiler_params=pltpu.CompilerParams(vmem_limit_bytes=60 << 20),
         name="finish",
-    )(dn, up, wo, wq, wk, wv, table, token)
+    )(dn, up, qo, kv, table, token)
     return out[15], list(out[:6]) + [a.reshape(-1) for a in out[6:15]]
 
 
@@ -1424,17 +1528,17 @@
     return result.astype(jnp.bfloat16), token_grad.astype(jnp.bfloat16), [total(g) for g in grads + vectors]
 
 
-def tuned_line(inputs, mats, vecs, cotangent, codes, own_codes, nb):
-    out = forward(inputs, codes, own_codes, mats, vecs, nb)
+def tuned_line(inputs, mats, vecs, cotangent, seg, live, nb):
+    out = forward(inputs, seg, live, mats, vecs, nb)
     wq, wk, wv, wo, wup, wdn, q_all, k_all, v_all, summed, attended, lse, table, bup = out
     out = middle(attended, inputs, cotangent, summed, lse, table, bup, wo, wup, wdn)
     result, rest, do, stats, delta, table, gdn, gup, gwo = out
     width = inputs.shape[1]
     early = [g.reshape(2, 2, 2, -1, width) for g in (gdn, gup, gwo)]
-    token_grad, table, rdn, rup, ro, rwq, rwk, rwv = backward(
-        codes, own_codes, do, stats, lse, delta, inputs, rest, table, q_all, k_all, v_all, [wq, wk, wv], early, nb,
+    token_grad, table, rdn, rup, rqo, rkv = backward(
+        seg, live, do, stats, lse, delta, inputs, rest, table, q_all, k_all, v_all, [wq, wk, wv], early, nb,
     )
-    token_grad, sums = finish(rdn, rup, ro, rwq, rwk, rwv, table, token_grad, vecs[8].shape[0])
+    token_grad, sums = finish(rdn, rup, rqo, rkv, table, token_grad, vecs[8].shape[0])
     return result, token_grad, sums
 
 
@@ -1453,7 +1557,7 @@
     mats = [query_weight, key_weight, value_weight, out_weight, up_weight, down_weight]
     vecs = [query_bias, value_bias, out_bias, first_gain, first_shift, down_bias, second_gain, second_shift, up_bias]
     if tuned_plane():
-        result, token_grad, sums = tuned_line(inputs, mats, vecs, cotangent[0], codes, own_codes, nb)
+        result, token_grad, sums = tuned_line(inputs, mats, vecs, cotangent[0], segments, live_mask, nb)
     else:
         result, token_grad, sums = whole_line(
             inputs, seg, live, mats, vecs, cotangent[0], codes, own_codes, start

time: 261 us -> 251 us (0.962)
  Pallas kernels: 254 us -> 247 us
  other arithmetic: 4.08 us -> 1.25 us
    pallas_call x1, Pallas kernels: 128 us -> 123 us  [backward(): pl.pallas_call(functools.partial(backward_kernel, nb), out_shape=(jax.Sha...]
where the time goes in v1:
time: 251 us
  Pallas kernels  247 us (98%)
    pallas_call x1, Pallas kernels, backward(): pl.pallas_call(functools.partial(backward_kernel, nb), out_shape=(jax.Sha...  123 us
    pallas_call x1, Pallas kernels, forward(): pl.pallas_call(functools.partial(forward_kernel, nb), out_shape=(*mats, e...  79.4 us
    pallas_call x1, Pallas kernels, middle(): pl.pallas_call(middle_kernel, out_shape=(S((n, width), bf), S((n, width),...  40.8 us

profile of v1, /device:TPU:0, one launch (start us, length us, event | category | flops | bytes accessed | tf_op | source)
XLA Modules:
  0.0 250.6 jit_solution(8383074193834579243)
XLA Ops:
  0.7 1.2 reshape.105.refs_17_
  1.9 79.4 %forward.1 = (bf16[768,768]{1,0:T(8,128)(2,1)}, bf16[768,768]{1,0:T(8,128)(2,1)}, bf16[768,768]{1,0:T(8,128)(2,1)}, bf16[768,768]{1,0:T(8,128)(2,1)}, bf16[768,3...) custom-call(bf16[512,768]{1,0:T(8,128)(2,1)} %bitcast.23, ...), custom_call_target="tpu_custom_call" | custom-call | tf_op jit(solution)/shard_map/forward/pallas_call | solution.py:896
  81.3 40.8 %middle.1 = (bf16[512,768]{1,0:T(8,128)(2,1)}, f32[512,768]{1,0:T(8,128)}, bf16[512,768]{1,0:T(8,128)(2,1)}, f32[6,8,512]{2,1,0:T(8,128)}, f32[512,768]{1,0:T(8,...) custom-call(bf16[512,768]{1,0:T(8,128)(2,1)} %get-tuple-element.62.a, ...), custom_call_target="tpu_custom_call" | custom-call | tf_op jit(solution)/shard_map/middle/pallas_call | solution.py:1097
  122.1 123.2 %backward.1 = (bf16[512,768]{1,0:T(8,128)(2,1)}, f32[16,768]{1,0:T(8,128)}, bf16[384,768]{1,0:T(8,128)(2,1)}, bf16[384,768]{1,0:T(8,128)(2,1)}, bf16[192,768]{1,0:T(8,128)(2,1)}, /*index=5*/bf16[192,768]{1,0:T(8,128)(2,1)}) custom-call(s32[1,2048]{1,0:T(1,128)} %refs_0_.1, s32[1,2048]{1,0:T(1,128)} %refs_1_.3, bf16[512,768]{1,0:T(8,128)(2,1)} %get-tuple-element.71.refs_2_, ...), custom_call_target="tpu_custom_call" | custom-call | tf_op jit(solution)/shard_map/backward/pallas_call | solution.py:1360
  245.3 4.0 %finish.1 = (f32[96,768]{1,0:T(8,128)}, f32[96,768]{1,0:T(8,128)}, f32[96,768]{1,0:T(8,128)}, f32[96,768]{1,0:T(8,128)}, f32[384,768]{1,0:T(8,128)}, /*index=5*/...) custom-call(bf16[384,768]{1,0:T(8,128)(2,1)} %get-tuple-element.85.d, ...), custom_call_target="tpu_custom_call" | custom-call | tf_op jit(solution)/shard_map/finish/pallas_call | solution.py:1422
  249.3 1.2 reduce

commit v2 on v1

--- a/solution.py
+++ b/solution.py
@@ -1008,7 +1008,7 @@
             total = total + dot(low, wdn[at, :], 1, 0)
         dh_ref[...] = total
         return 0
-    lax.fori_loop(0, chunks, up, 0)
+    lax.fori_loop(0, chunks, up, 0, unroll=True)
 
     def second(i, _):
         r = rows_of(i)
@@ -1047,7 +1047,7 @@
         pltpu.make_async_copy(gdn.at[at], gdn_hbm.at[at], osems.at[0, t]).start()
         pltpu.make_async_copy(gup.at[:, t], gup_hbm.at[:, t], osems.at[1, t]).start()
         return 0
-    lax.fori_loop(0, chunks, down, 0)
+    lax.fori_loop(0, chunks, down, 0, unroll=True)
 
     def third(i, _):
         r = rows_of(i)

time: 251 us -> 253 us (level)
  the two profiles are of different devices: /device:TPU:0 before, /device:TPU:25 now
where the time goes in v2:
time: 253 us; the launch traced here: 248 us
  Pallas kernels  245 us (97%)
    pallas_call x1, Pallas kernels, backward(): pl.pallas_call(functools.partial(backward_kernel, nb), out_shape=(jax.Sha...  127 us
    pallas_call x1, Pallas kernels, forward(): pl.pallas_call(functools.partial(forward_kernel, nb), out_shape=(*mats, e...  75.9 us
    pallas_call x1, Pallas kernels, middle(): pl.pallas_call(middle_kernel, out_shape=(S((n, width), bf), S((n, width),...  37.5 us

profile of v2, /device:TPU:25, one launch (start us, length us, event | category | flops | bytes accessed | tf_op | source)
XLA Modules:
  0.0 248.2 jit_solution(17504834811197845352)
XLA Ops:
  0.7 1.2 reshape.105.refs_17_
  1.9 75.9 %forward.1 = (bf16[768,768]{1,0:T(8,128)(2,1)}, bf16[768,768]{1,0:T(8,128)(2,1)}, bf16[768,768]{1,0:T(8,128)(2,1)}, bf16[768,768]{1,0:T(8,128)(2,1)}, bf16[768,3...) custom-call(bf16[512,768]{1,0:T(8,128)(2,1)} %bitcast.23, ...), custom_call_target="tpu_custom_call" | custom-call | tf_op jit(solution)/shard_map/forward/pallas_call | solution.py:896
  77.8 37.5 %middle.1 = (bf16[512,768]{1,0:T(8,128)(2,1)}, f32[512,768]{1,0:T(8,128)}, bf16[512,768]{1,0:T(8,128)(2,1)}, f32[6,8,512]{2,1,0:T(8,128)}, f32[512,768]{1,0:T(8,...) custom-call(bf16[512,768]{1,0:T(8,128)(2,1)} %get-tuple-element.62.a, ...), custom_call_target="tpu_custom_call" | custom-call | tf_op jit(solution)/shard_map/middle/pallas_call | solution.py:1097
  115.3 127.2 %backward.1 = (bf16[512,768]{1,0:T(8,128)(2,1)}, f32[16,768]{1,0:T(8,128)}, bf16[384,768]{1,0:T(8,128)(2,1)}, bf16[384,768]{1,0:T(8,128)(2,1)}, bf16[192,768]{1,0:T(8,128)(2,1)}, /*index=5*/bf16[192,768]{1,0:T(8,128)(2,1)}) custom-call(s32[1,2048]{1,0:T(1,128)} %refs_0_.1, s32[1,2048]{1,0:T(1,128)} %refs_1_.3, bf16[512,768]{1,0:T(8,128)(2,1)} %get-tuple-element.71.refs_2_, ...), custom_call_target="tpu_custom_call" | custom-call | tf_op jit(solution)/shard_map/backward/pallas_call | solution.py:1360
  242.4 4.0 %finish.1 = (f32[96,768]{1,0:T(8,128)}, f32[96,768]{1,0:T(8,128)}, f32[96,768]{1,0:T(8,128)}, f32[96,768]{1,0:T(8,128)}, f32[384,768]{1,0:T(8,128)}, /*index=5*/...) custom-call(bf16[384,768]{1,0:T(8,128)(2,1)} %get-tuple-element.85.d, ...), custom_call_target="tpu_custom_call" | custom-call | tf_op jit(solution)/shard_map/finish/pallas_call | solution.py:1422
  246.5 1.2 reduce

commit v3 on v2

--- a/solution.py
+++ b/solution.py
@@ -1008,7 +1008,7 @@
             total = total + dot(low, wdn[at, :], 1, 0)
         dh_ref[...] = total
         return 0
-    lax.fori_loop(0, chunks, up, 0, unroll=True)
+    lax.fori_loop(0, chunks, up, 0, unroll=2)
 
     def second(i, _):
         r = rows_of(i)
@@ -1047,7 +1047,7 @@
         pltpu.make_async_copy(gdn.at[at], gdn_hbm.at[at], osems.at[0, t]).start()
         pltpu.make_async_copy(gup.at[:, t], gup_hbm.at[:, t], osems.at[1, t]).start()
         return 0
-    lax.fori_loop(0, chunks, down, 0, unroll=True)
+    lax.fori_loop(0, chunks, down, 0, unroll=2)
 
     def third(i, _):
         r = rows_of(i)

time: 253 us -> 249 us (0.984)
  the two profiles are of different devices: /device:TPU:25 before, /device:TPU:0 now
where the time goes in v3:
time: 249 us
  Pallas kernels  245 us (98%)
    pallas_call x1, Pallas kernels, backward(): pl.pallas_call(functools.partial(backward_kernel, nb), out_shape=(jax.Sha...  123 us
    pallas_call x1, Pallas kernels, forward(): pl.pallas_call(functools.partial(forward_kernel, nb), out_shape=(*mats, e...  79.4 us
    pallas_call x1, Pallas kernels, middle(): pl.pallas_call(middle_kernel, out_shape=(S((n, width), bf), S((n, width),...  38.7 us

profile of v3, /device:TPU:0, one launch (start us, length us, event | category | flops | bytes accessed | tf_op | source)
XLA Modules:
  0.0 248.6 jit_solution(16353849231175573294)
XLA Ops:
  0.7 1.2 reshape.105.refs_17_
  1.9 79.4 %forward.1 = (bf16[768,768]{1,0:T(8,128)(2,1)}, bf16[768,768]{1,0:T(8,128)(2,1)}, bf16[768,768]{1,0:T(8,128)(2,1)}, bf16[768,768]{1,0:T(8,128)(2,1)}, bf16[768,3...) custom-call(bf16[512,768]{1,0:T(8,128)(2,1)} %bitcast.23, ...), custom_call_target="tpu_custom_call" | custom-call | tf_op jit(solution)/shard_map/forward/pallas_call | solution.py:896
  81.3 38.7 %middle.1 = (bf16[512,768]{1,0:T(8,128)(2,1)}, f32[512,768]{1,0:T(8,128)}, bf16[512,768]{1,0:T(8,128)(2,1)}, f32[6,8,512]{2,1,0:T(8,128)}, f32[512,768]{1,0:T(8,...) custom-call(bf16[512,768]{1,0:T(8,128)(2,1)} %get-tuple-element.62.a, ...), custom_call_target="tpu_custom_call" | custom-call | tf_op jit(solution)/shard_map/middle/pallas_call | solution.py:1097
  120.1 123.2 %backward.1 = (bf16[512,768]{1,0:T(8,128)(2,1)}, f32[16,768]{1,0:T(8,128)}, bf16[384,768]{1,0:T(8,128)(2,1)}, bf16[384,768]{1,0:T(8,128)(2,1)}, bf16[192,768]{1,0:T(8,128)(2,1)}, /*index=5*/bf16[192,768]{1,0:T(8,128)(2,1)}) custom-call(s32[1,2048]{1,0:T(1,128)} %refs_0_.1, s32[1,2048]{1,0:T(1,128)} %refs_1_.3, bf16[512,768]{1,0:T(8,128)(2,1)} %get-tuple-element.71.refs_2_, ...), custom_call_target="tpu_custom_call" | custom-call | tf_op jit(solution)/shard_map/backward/pallas_call | solution.py:1360
  243.3 4.0 %finish.1 = (f32[96,768]{1,0:T(8,128)}, f32[96,768]{1,0:T(8,128)}, f32[96,768]{1,0:T(8,128)}, f32[96,768]{1,0:T(8,128)}, f32[384,768]{1,0:T(8,128)}, /*index=5*/...) custom-call(bf16[384,768]{1,0:T(8,128)(2,1)} %get-tuple-element.85.d, ...), custom_call_target="tpu_custom_call" | custom-call | tf_op jit(solution)/shard_map/finish/pallas_call | solution.py:1422
  247.3 1.2 reduce
